TPU v7x, 128 devices: a whole 4x4x4 slice. The times are simulated.
128 devices in a mesh: docs: 128 (over y, x, z, core).
Axes of the slice: x: 4, y: 4, z: 4, core: 2. Of those that a mesh axis runs over, the one named last changes fastest.
Arguments:
- block_count_values: int32 [5120, 256, 256], P('docs'), may hold values from 1 to 15
- word_factor: bfloat16 [262144, 512], P('docs'), may hold values from 0.029907227 to 0.29882812
- doc_factor: bfloat16 [512, 262144], P(None, 'docs'), may hold values from 0.029907227 to 0.29882812
- block_word: int32 [5120], P('docs'), may hold values from 0 to 1023, as said below
- block_docs: int32 [5120], P('docs'), may hold values from 0 to 7
- block_count: int32 [128], P('docs'), may hold values from 5 to 40
Outputs:
- word_gradient: float32 [262144, 512], P('docs')
- document_gradient: float32 [512, 262144], P(None, 'docs')
Inputs may be any that keep to these rules, and one draw needn't show every extreme that they name: `block_word`: on device d every slot names a word block from (d - 1) * 8 to (d + 2) * 8 - 1, taken modulo 1024; the pairs of word block and document block of one device's slots are all different.
All inputs are finite; a program needn't handle non-finite values.
Results may differ from a plain program's by a relative error of at most 0.00038.
Values may be sent and summed in bfloat16 or wider, within the bound.
No kernel may reach another device: no remote copies, remote signals or barrier semaphores. Data moves between devices by JAX's collectives and lax.ppermute only.
A program may use at most 128 MiB of HBM per device.

v0:
```python
import functools

import jax
import jax.numpy as jnp
from jax import lax
from jax.experimental import pallas as pl
from jax.experimental.pallas import tpu as pltpu
from jax.sharding import PartitionSpec as P

F32 = jnp.float32
BF16 = jnp.bfloat16
F16 = jnp.float16
VMEM = pl.BlockSpec(memory_space=pltpu.VMEM)
SMEM = pl.BlockSpec(memory_space=pltpu.SMEM)
HBM = pl.BlockSpec(memory_space=pltpu.HBM)
DEAD = 1 << 10
GROUP = 4
RING = 2 * GROUP
CHEAP = pl.CostEstimate(flops=1, bytes_accessed=1, transcendentals=0)


def params(megabytes):
    return pltpu.CompilerParams(vmem_limit_bytes=megabytes << 20)


def block_at(index, edge):
    return pl.ds(pl.multiple_of(index * edge, edge), edge)


def code_parts(code):
    return code & 63, (code >> 6) & 15, code >> 10


def word_kernel(spec, order, bounds, counts, words, docs, *refs):
    edge, first_mark, last_mark, base, chained = spec
    if chained:
        refs = refs[1:]
    grad, kept, held, staged, sems, out_sems = refs
    first, last = bounds[first_mark], bounds[last_mark]

    def fetch(place):
        slot, _, _ = code_parts(order[place])
        return pltpu.make_async_copy(counts.at[slot], held.at[place], sems.at[place])

    def keep(place, spot):
        return pltpu.make_async_copy(staged.at[spot], kept.at[place], out_sems.at[spot])

    @pl.loop(first, last)
    def _(place):
        fetch(place).start()

    grad[...] = jnp.zeros_like(grad)

    @pl.loop(0, (last - first + GROUP - 1) // GROUP)
    def _(step):
        start = first + GROUP * step

        @pl.loop(start, jnp.minimum(start + GROUP, last))
        def _(place):
            fetch(place).wait()

        half = (step & 1) * GROUP

        @pl.when(step > 1)
        def _():
            for g in range(GROUP):
                keep(start + g - 2 * GROUP, half + g).wait()

        places = [jnp.minimum(start + g, last - 1) for g in range(GROUP)]
        parts = [code_parts(order[place]) for place in places]
        rows = [block_at(word, edge) for _, word, _ in parts]
        sums = [block_at(word - base, edge) for _, word, _ in parts]
        cols = [block_at(doc, edge) for _, _, doc in parts]
        products = [
            jnp.dot(words[r, :], docs[:, c], preferred_element_type=F32) for r, c in zip(rows, cols)
        ]
        excess = []
        for g in range(GROUP):
            ratio = held[places[g]].astype(F32) / products[g]
            one = (1.0 - ratio).astype(BF16)
            if g:
                one = jnp.where(start + g < last, one, jnp.zeros_like(one))
            excess.append(one)
            staged[half + g] = one
        terms = [
            lax.dot_general(e, docs[:, c], (((1,), (1,)), ((), ())), preferred_element_type=F32)
            for e, c in zip(excess, cols)
        ]
        for g in range(GROUP):
            grad[sums[g], :] += terms[g]

        @pl.loop(start, jnp.minimum(start + GROUP, last))
        def _(place):
            keep(place, half + place - start).start()

    steps = (last - first + GROUP - 1) // GROUP

    @pl.loop(first + GROUP * jnp.maximum(steps - 2, 0), last)
    def _(place):
        keep(place, (place - first) & (RING - 1)).wait()


def word_terms(name, order, bounds, counts, words, docs, marks, part=None, kept=None):
    slots, edge, _ = counts.shape
    chained = kept is not None
    low, high = part or (0, words.shape[0] // edge)
    spec = (edge, marks[0], marks[1], low, chained)
    return pl.pallas_call(
        functools.partial(word_kernel, spec),
        out_shape=[
            jax.ShapeDtypeStruct(((high - low) * edge, words.shape[1]), F32),
            jax.ShapeDtypeStruct((slots, edge, edge), BF16),
        ],
        in_specs=[SMEM, SMEM, HBM, VMEM, VMEM] + [HBM] * chained,
        out_specs=[VMEM, HBM],
        scratch_shapes=[
            pltpu.VMEM((slots, edge, edge), counts.dtype),
            pltpu.VMEM((RING, edge, edge), BF16),
            pltpu.SemaphoreType.DMA((slots,)),
            pltpu.SemaphoreType.DMA((RING,)),
        ],
        input_output_aliases={5: 1} if chained else {},
        compiler_params=params(20),
        cost_estimate=CHEAP,
        name=name,
    )(order, bounds, counts, words, docs, *([kept] if chained else []))


def doc_kernel(spec, order, bounds, kept, *refs):
    edge, marks = spec
    sides, grad, held, sems = refs[:-3], refs[-3], refs[-2], refs[-1]
    total = bounds[marks[-1]]

    def fetch(place):
        return pltpu.make_async_copy(kept.at[place], held.at[place], sems.at[place])

    @pl.loop(0, total)
    def _(place):
        fetch(place).start()

    grad[...] = jnp.zeros_like(grad)
    for words, first_mark, last_mark in zip(sides, marks, marks[1:]):
        first, last = bounds[first_mark], bounds[last_mark]

        @pl.loop(0, (last - first + GROUP - 1) // GROUP)
        def _(step, words=words, first=first, last=last):
            start = first + GROUP * step

            @pl.loop(start, jnp.minimum(start + GROUP, last))
            def _(place):
                fetch(place).wait()

            places = [jnp.minimum(start + g, last - 1) for g in range(GROUP)]
            parts = [code_parts(order[place]) for place in places]
            cols = [block_at(doc, edge) for _, _, doc in parts]
            terms = []
            for g in range(GROUP):
                one = held[places[g]]
                if g:
                    one = jnp.where(start + g < last, one, jnp.zeros_like(one))
                rows = block_at(parts[g][1], edge)
                terms.append(
                    lax.dot_general(
                        words[rows, :], one, (((0,), (0,)), ((), ())), preferred_element_type=F32
                    )
                )
            for c, term in zip(cols, terms):
                grad[:, c] += term


def doc_terms(order, bounds, kept, sides, marks, width):
    slots, edge, _ = kept.shape
    rank = sides[0].shape[1]
    return pl.pallas_call(
        functools.partial(doc_kernel, (edge, marks)),
        out_shape=jax.ShapeDtypeStruct((rank, width), F32),
        in_specs=[SMEM, SMEM, HBM] + [VMEM] * len(sides),
        out_specs=VMEM,
        scratch_shapes=[pltpu.VMEM((slots, edge, edge), BF16), pltpu.SemaphoreType.DMA((slots,))],
        compiler_params=params(16),
        cost_estimate=CHEAP,
        name="docs",
    )(order, bounds, kept, *sides)


def finish_kernel(start, pieces, chained, *refs):
    own, near, far = refs[:3]
    out, sums, sems = refs[-3:]
    rows = far.shape[0] // pieces
    copies = []
    for piece in range(pieces):
        here = pl.ds(piece * rows, rows)
        there = pl.ds(start + piece * rows, rows)
        sums[here, :] = own[there, :] + near[there, :] + far[here, :]
        copies.append(pltpu.make_async_copy(sums.at[here], out.at[there], sems.at[piece]))
        copies[-1].start()
    for copy in copies:
        copy.wait()


def finish(name, own, near, far, start, result=None):
    chained = result is not None
    pieces = 4
    return pl.pallas_call(
        functools.partial(finish_kernel, start, pieces, chained),
        out_shape=jax.ShapeDtypeStruct(own.shape, F32),
        in_specs=[VMEM] * 3 + [HBM] * chained,
        out_specs=HBM,
        scratch_shapes=[pltpu.VMEM(far.shape, F32), pltpu.SemaphoreType.DMA((pieces,))],
        input_output_aliases={3: 0} if chained else {},
        compiler_params=params(16),
        cost_estimate=CHEAP,
        name=name,
    )(own, near, far, *([result] if chained else []))


def slot_order(block_word, block_docs, live, position, own_blocks, devices):
    slot = jnp.arange(block_word.shape[0], dtype=jnp.int32)
    local = jnp.mod(block_word - (position - 1) * own_blocks, own_blocks * devices)
    side = local // own_blocks
    inner = local - side * own_blocks
    even = position % 2 == 0
    group = jnp.where(side == 1, 0, jnp.where((side == 0) == even, 2, 1))
    key = jnp.where(slot < live, group * own_blocks + inner, DEAD)
    rank_key = key * 64 + slot
    rank = jnp.sum((rank_key[None, :] < rank_key[:, None]).astype(jnp.int32), axis=1)
    code = slot + inner * 64 + block_docs * 1024
    order = jnp.sum(jnp.where(rank[:, None] == slot[None, :], code[:, None], 0), axis=0)
    marks = jnp.arange(3 * own_blocks + 1, dtype=jnp.int32)
    bounds = jnp.sum((key[None, :] < marks[:, None]).astype(jnp.int32), axis=1)
    return order, bounds


def on_device(block_count_values, word_factor, doc_factor, block_word, block_docs, block_count):
    devices = lax.axis_size("docs")
    position = lax.axis_index("docs")
    edge = block_count_values.shape[1]
    rows = word_factor.shape[0]
    own_blocks = rows // edge
    split = own_blocks // 2
    half = split * edge
    marks = (0, own_blocks, 2 * own_blocks, 2 * own_blocks + split, 3 * own_blocks)
    partner_route = [(i, i ^ 1) for i in range(devices)]
    cross_route = [(i, (i + 1) % devices if i % 2 else (i - 1) % devices) for i in range(devices)]

    def across(block):
        return lax.ppermute(block, "docs", cross_route)

    there = across(word_factor)
    partner = lax.ppermute(word_factor, "docs", partner_route)
    order, bounds = slot_order(
        block_word, block_docs, block_count[0], position, own_blocks, devices
    )
    counts = pltpu.with_memory_space_constraint(block_count_values, pltpu.HBM)
    run = functools.partial(word_terms, bounds=bounds, counts=counts, docs=doc_factor)
    own, kept = run("own", order=order, words=word_factor, marks=marks[0:2])
    near, kept = run("partner", order=order, words=partner, marks=marks[1:3], kept=kept)
    order, near = lax.optimization_barrier((order, near))
    near = lax.ppermute(near, "docs", partner_route)
    far_a, kept = run("cross_a", order=order, words=there, marks=marks[2:4], kept=kept, part=(0, split))
    order, far_a = lax.optimization_barrier((order, far_a.astype(F16)))
    far_a = across(far_a)
    far_b, kept = run(
        "cross_b", order=order, words=there, marks=marks[3:5], kept=kept, part=(split, own_blocks)
    )
    order, far_b, far_a = lax.optimization_barrier((order, far_b.astype(F16), far_a))
    far_b = across(far_b)
    document_gradient = doc_terms(
        order,
        bounds,
        kept,
        (word_factor, partner, there),
        (0, own_blocks, 2 * own_blocks, 3 * own_blocks),
        doc_factor.shape[1],
    )
    document_gradient, near = lax.optimization_barrier((document_gradient, near))
    result = finish("finish_a", own, near, far_a.astype(F32), 0)
    result, far_b = lax.optimization_barrier((result, far_b))
    result = finish("finish_b", own, near, far_b.astype(F32), half, result)
    return (result, document_gradient)


def solution(mesh):
    placed = (
        P("docs", None, None),
        P("docs", None),
        P(None, "docs"),
        P("docs"),
        P("docs"),
        P("docs"),
    )
    return jax.shard_map(
        on_device,
        mesh=mesh,
        in_specs=placed,
        out_specs=(P("docs", None), P(None, "docs")),
        check_vma=False,
    )
```

profile of v0, /device:TPU:0, one launch (start us, length us, event | category | flops | bytes accessed | tf_op | source)
XLA Modules:
  0.0 79.6 jit_solution(7550636589078128208)
XLA Ops:
  0.6 0.1 collective-permute-start
  0.7 8.9 %collective-permute-start.1 = (bf16[2048,512]{1,0:T(8,128)(2,1)}, bf16[2048,512]{1,0:T(8,128)(2,1)S(1)}, u32[]{:S(2)}, u32[]{:S(2)}) collective-permute-start(bf16[2048,512]{1,0:T(8,128)(2,1)} %refs_0_.1), channel_id=1, source_target_pairs={{0,127},{1,2},{2,1},{3,4},{4,3},{5,6},{6,5},{7,8},{8,7},{9,10},{10... | collective-permute-start | bytes 6291464 | tf_op jit(solution)/shard_map/ppermute | solution.py:247
  10.2 0.7 iota_add_fusion
  10.9 0.1 convert_reduce_fusion.1.bounds
  11.0 0.2 convert_reduce_fusion
  11.2 0.7 multiply_add_fusion
  11.9 0.1 select_reduce_fusion.order
  12.0 1.6 %copy-done = bf16[512,2048]{1,0:T(8,128)(2,1)S(1)} copy-done((bf16[512,2048]{1,0:T(8,128)(2,1)S(1)}, bf16[512,2048]{1,0:T(8,128)(2,1)}, u32[]{:S(2)}) %copy-start) | copy-done | bytes 2097176
  13.6 1.6 %copy-done.1 = bf16[2048,512]{1,0:T(8,128)(2,1)S(1)} copy-done((bf16[2048,512]{1,0:T(8,128)(2,1)S(1)}, bf16[2048,512]{1,0:T(8,128)(2,1)}, u32[]{:S(2)}) %copy-start.1) | copy-done | bytes 2097176
  15.2 5.1 %own.1 = (f32[2048,512]{1,0:T(8,128)S(1)}, bf16[40,256,256]{2,1,0:T(8,128)(2,1)S(1)}) custom-call(s32[40]{0:T(128)S(1)} %select_reduce_fusion.order, s32[25]{0:T(128)S(1)} %convert_reduce_fusion.1.bounds, s32[40,256,256]{2,1,0:T(8,128)} %counts.7, bf16[2048,512]{1,0:T(8,128)(2,1)S(1)} %copy-done.1, bf16[512,2048]{1,0:T(8,128)(2,1)S(1)} %copy-done), custom_call_target="tpu_custom_call" | custom-call | flops 1 | bytes 1 | tf_op jit(solution)/shard_map/own/pallas_call | solution.py:108
  20.3 5.8 %partner.1 = (f32[2048,512]{1,0:T(8,128)S(1)}, bf16[40,256,256]{2,1,0:T(8,128)(2,1)S(1)}) custom-call(s32[40]{0:T(128)S(1)} %select_reduce_fusion.order, s32[25]{0:T(128)S(1)} %convert_reduce_fusion.1.bounds, s32[40,256,256]{2,1,0:T(8,128)} %counts.7, bf16[2048,512]{1,0:T(8,128)(2,1)} %collective-permute-done.words.refs_1_, ...), custom_call_target="tpu_custom_call", output_to_operand_aliasing={{1}: (5, {})} | custom-call | flops 1 | bytes 1 | tf_op jit(solution)/shard_map/partner/pallas_call | solution.py:108
  26.2 7.3 %collective-permute-done.1.words.refs_2_ = bf16[2048,512]{1,0:T(8,128)(2,1)S(1)} collective-permute-done((bf16[2048,512]{1,0:T(8,128)(2,1)}, bf16[2048,512]{1,0:T(8,128)(2,1)S(1)}, u32[]{:S(2)}, u32[]{:S(2)}) %collective-permute-start.1) | collective-permute-done | bytes 2097184 | tf_op jit(solution)/shard_map/ppermute | solution.py:247
  33.5 3.2 %cross_a.1 = (f32[1024,512]{1,0:T(8,128)S(1)}, bf16[40,256,256]{2,1,0:T(8,128)(2,1)S(1)}) custom-call(s32[40]{0:T(128)S(1)} %select_reduce_fusion.order, s32[25]{0:T(128)S(1)} %convert_reduce_fusion.1.bounds, s32[40,256,256]{2,1,0:T(8,128)} %counts.7, bf16[2048,512]{1,0:T(8,128)(2,1)S(1)} %collective-permute-done.1.words.refs_2_, ...), custom_call_target="tpu_custom_call", output_to_operand_aliasing={{1}: (5, {})} | custom-call | flops 1 | bytes 1 | tf_op jit(solution)/shard_map/cross_a/pallas_call | solution.py:108
  36.7 0.3 convert_element_type.20
  37.0 8.8 %collective-permute-start.2 = (f16[1024,512]{1,0:T(8,128)(2,1)S(1)}, f16[1024,512]{1,0:T(8,128)(2,1)S(1)}, u32[]{:S(2)}, u32[]{:S(2)}) collective-permute-start(f16[1024,512]{1,0:T(8,128)(2,1)S(1)} %convert_element_type.20), channel_id=1, source_target_pairs={{0,127},{1,2},{2,1},{3,4},{4,3},{5,6},{6,5},{7,8},{8,7},{9,10},{10... | collective-permute-start | bytes 3145736 | tf_op jit(solution)/shard_map/ppermute | solution.py:247
  45.8 3.4 %cross_b.1 = (f32[1024,512]{1,0:T(8,128)S(1)}, bf16[40,256,256]{2,1,0:T(8,128)(2,1)S(1)}) custom-call(s32[40]{0:T(128)S(1)} %select_reduce_fusion.order, s32[25]{0:T(128)S(1)} %convert_reduce_fusion.1.bounds, s32[40,256,256]{2,1,0:T(8,128)} %counts.7, bf16[2048,512]{1,0:T(8,128)(2,1)S(1)} %collective-permute-done.1.words.refs_2_, ...), custom_call_target="tpu_custom_call", output_to_operand_aliasing={{1}: (5, {})} | custom-call | flops 1 | bytes 1 | tf_op jit(solution)/shard_map/cross_b/pallas_call | solution.py:108
  49.2 0.3 convert_element_type.21
  49.5 8.8 %collective-permute-done.2 = f16[1024,512]{1,0:T(8,128)(2,1)S(1)} collective-permute-done((f16[1024,512]{1,0:T(8,128)(2,1)S(1)}, f16[1024,512]{1,0:T(8,128)(2,1)S(1)}, u32[]{:S(2)}, u32[]{:S(2)}) %collective-permute-start.2) | collective-permute-done | bytes 1048608 | tf_op jit(solution)/shard_map/ppermute | solution.py:247
  58.2 7.2 %collective-permute-start.4 = (f16[1024,512]{1,0:T(8,128)(2,1)S(1)}, f16[1024,512]{1,0:T(8,128)(2,1)S(1)}, u32[]{:S(2)}, u32[]{:S(2)}) collective-permute-start(f16[1024,512]{1,0:T(8,128)(2,1)S(1)} %convert_element_type.21), channel_id=1, source_target_pairs={{0,127},{1,2},{2,1},{3,4},{4,3},{5,6},{6,5},{7,8},{8,7},{9,10},{10... | collective-permute-start | bytes 3145736 | tf_op jit(solution)/shard_map/ppermute | solution.py:247
  65.4 10.7 %docs.9 = f32[512,2048]{1,0:T(8,128)} custom-call(s32[40]{0:T(128)S(1)} %select_reduce_fusion.order, s32[25]{0:T(128)S(1)} %convert_reduce_fusion.1.bounds, bf16[40,256,256]{2,1,0:T(8,128)(2,1)S(1)} %get-tuple-element.32.kept, bf16[2048,512]{1,0:T(8,128)(2,1)S(1)} %copy-done.1, bf16[2048,512]{1,0:T(8,128)(2,1)} %collective-permute-done.words.refs_1_, ...), custom_call_target="tpu_custom_call" | custom-call | flops 1 | bytes 1 | tf_op jit(solution)/shard_map/docs/pallas_call | solution.py:174
  76.1 0.3 convert_element_type.22.refs_2_
  76.4 1.4 %finish_a.1.refs_3_ = f32[2048,512]{1,0:T(8,128)} custom-call(f32[2048,512]{1,0:T(8,128)S(1)} %get-tuple-element.21.refs_0_, f32[2048,512]{1,0:T(8,128)S(1)} %collective-permute-done.3.refs_1_, f32[1024,512]{1,0:T(8,128)S(1)} %convert_element_type.22.refs_2_), custom_call_target="tpu_custom_call" | custom-call | flops 1 | bytes 1 | tf_op jit(solution)/shard_map/finish_a/pallas_call | solution.py:204
  77.9 0.3 convert_element_type.23.refs_2_
  78.2 1.4 %finish_b.1 = f32[2048,512]{1,0:T(8,128)} custom-call(f32[2048,512]{1,0:T(8,128)S(1)} %get-tuple-element.21.refs_0_, f32[2048,512]{1,0:T(8,128)S(1)} %collective-permute-done.3.refs_1_, f32[1024,512]{1,0:T(8,128)S(1)} %convert_element_type.23.refs_2_, f32[2048,512]{1,0:T(8,128)} %finish_a.1.refs_3_), custom_call_target="tpu_custom_call", output_to_operand_aliasing={{}: (3, {})} | custom-call | flops 1 | bytes 1 | tf_op jit(solution)/shard_map/finish_b/pallas_call | solution.py:204
  (6 shorter events, 0.1 us)
Async XLA Ops:
  0.6 19.7 %collective-permute-start = (bf16[2048,512]{1,0:T(8,128)(2,1)}, bf16[2048,512]{1,0:T(8,128)(2,1)}, u32[]{:S(2)}, u32[]{:S(2)}) collective-permute-start(bf16[2048,512]{1,0:T(8,128)(2,1)} %refs_0_.1), channel_id=1, source_target_pairs={{0,1},{1,0},{2,3},{3,2},{4,5},{5,4},{6,7},{7,6},{8,9},{9,8},{10,11... | collective-permute-start | bytes 6291464 | tf_op jit(solution)/shard_map/ppermute | solution.py:250
  0.7 32.8 %collective-permute-start.1 = (bf16[2048,512]{1,0:T(8,128)(2,1)}, bf16[2048,512]{1,0:T(8,128)(2,1)S(1)}, u32[]{:S(2)}, u32[]{:S(2)}) collective-permute-start(bf16[2048,512]{1,0:T(8,128)(2,1)} %refs_0_.1), channel_id=1, source_target_pairs={{0,127},{1,2},{2,1},{3,4},{4,3},{5,6},{6,5},{7,8},{8,7},{9,10},{10... | collective-permute-start | bytes 6291464 | tf_op jit(solution)/shard_map/ppermute | solution.py:247
  12.0 1.6 %copy-start = (bf16[512,2048]{1,0:T(8,128)(2,1)S(1)}, bf16[512,2048]{1,0:T(8,128)(2,1)}, u32[]{:S(2)}) copy-start(bf16[512,2048]{1,0:T(8,128)(2,1)} %docs.8) | copy-start | bytes 6291460
  13.6 1.6 %copy-start.1 = (bf16[2048,512]{1,0:T(8,128)(2,1)S(1)}, bf16[2048,512]{1,0:T(8,128)(2,1)}, u32[]{:S(2)}) copy-start(bf16[2048,512]{1,0:T(8,128)(2,1)} %refs_0_.1) | copy-start | bytes 6291460
  26.1 50.3 %collective-permute-start.3 = (f32[2048,512]{1,0:T(8,128)S(1)}, f32[2048,512]{1,0:T(8,128)S(1)}, u32[]{:S(2)}, u32[]{:S(2)}) collective-permute-start(f32[2048,512]{1,0:T(8,128)S(1)} %get-tuple-element.33), channel_id=1, source_target_pairs={{0,1},{1,0},{2,3},{3,2},{4,5},{5,4},{6,7},{7,6},{8,9},{9,8},{10,11... | collective-permute-start | bytes 12582920 | tf_op jit(solution)/shard_map/ppermute | solution.py:259
  37.0 21.3 %collective-permute-start.2 = (f16[1024,512]{1,0:T(8,128)(2,1)S(1)}, f16[1024,512]{1,0:T(8,128)(2,1)S(1)}, u32[]{:S(2)}, u32[]{:S(2)}) collective-permute-start(f16[1024,512]{1,0:T(8,128)(2,1)S(1)} %convert_element_type.20), channel_id=1, source_target_pairs={{0,127},{1,2},{2,1},{3,4},{4,3},{5,6},{6,5},{7,8},{8,7},{9,10},{10... | collective-permute-start | bytes 3145736 | tf_op jit(solution)/shard_map/ppermute | solution.py:247
  58.2 19.7 %collective-permute-start.4 = (f16[1024,512]{1,0:T(8,128)(2,1)S(1)}, f16[1024,512]{1,0:T(8,128)(2,1)S(1)}, u32[]{:S(2)}, u32[]{:S(2)}) collective-permute-start(f16[1024,512]{1,0:T(8,128)(2,1)S(1)} %convert_element_type.21), channel_id=1, source_target_pairs={{0,127},{1,2},{2,1},{3,4},{4,3},{5,6},{6,5},{7,8},{8,7},{9,10},{10... | collective-permute-start | bytes 3145736 | tf_op jit(solution)/shard_map/ppermute | solution.py:247
where the time goes:
time: 80.1 us; the launch traced here: 79.6 us
  Pallas kernels  31.1 us (39%)
  starting transfers between devices  25 us (31%)
  waiting for transfers between devices  16.1 us (20%)
  local copies, waits for them, and re-layouts  3.18 us (4%)
  other arithmetic  2.81 us (4%)
  between operations  1.4 us (2%)
    ppermute x3, starting transfers between devices, across(): return lax.ppermute(block, 'docs', cross_route)  24.8 us
    pallas_call x4, Pallas kernels, word_terms(): pl.pallas_call(functools.partial(word_kernel, spec), out_shape=[jax.Shape...  17.5 us
    ppermute x3, waiting for transfers between devices, across(): return lax.ppermute(block, 'docs', cross_route)  16.1 us
    pallas_call x1, Pallas kernels, doc_terms(): pl.pallas_call(functools.partial(doc_kernel, (edge, marks)), out_shape=ja...  10.7 us
    unnamed x4, local copies, waits for them, and re-layouts  3.18 us
    pallas_call x2, Pallas kernels, finish(): pl.pallas_call(functools.partial(finish_kernel, start, pieces, chained),...  2.88 us
  transfers between devices with their start and end apart: 5, of which 2 were waited for; matrix products, arithmetic and copies ran while one was open for 3% of the time, Pallas kernels for 37%

commit v1 on v0

--- a/solution.py
+++ b/solution.py
@@ -38,36 +38,35 @@
     grad, kept, held, staged, sems, out_sems = refs
     first, last = bounds[first_mark], bounds[last_mark]
 
+    top = order.shape[0] - 1
+    steps = (last - first + GROUP - 1) // GROUP
+
     def fetch(place):
-        slot, _, _ = code_parts(order[place])
+        slot, _, _ = code_parts(order[jnp.minimum(place, top)])
         return pltpu.make_async_copy(counts.at[slot], held.at[place], sems.at[place])
 
     def keep(place, spot):
         return pltpu.make_async_copy(staged.at[spot], kept.at[place], out_sems.at[spot])
 
-    @pl.loop(first, last)
+    @pl.loop(first, first + steps * GROUP)
     def _(place):
         fetch(place).start()
 
     grad[...] = jnp.zeros_like(grad)
 
-    @pl.loop(0, (last - first + GROUP - 1) // GROUP)
+    @pl.loop(0, steps)
     def _(step):
         start = first + GROUP * step
-
-        @pl.loop(start, jnp.minimum(start + GROUP, last))
-        def _(place):
-            fetch(place).wait()
-
         half = (step & 1) * GROUP
+        for g in range(GROUP):
+            fetch(start + g).wait()
 
         @pl.when(step > 1)
         def _():
             for g in range(GROUP):
                 keep(start + g - 2 * GROUP, half + g).wait()
 
-        places = [jnp.minimum(start + g, last - 1) for g in range(GROUP)]
-        parts = [code_parts(order[place]) for place in places]
+        parts = [code_parts(order[jnp.minimum(start + g, last - 1)]) for g in range(GROUP)]
         rows = [block_at(word, edge) for _, word, _ in parts]
         sums = [block_at(word - base, edge) for _, word, _ in parts]
         cols = [block_at(doc, edge) for _, _, doc in parts]
@@ -76,7 +75,7 @@
         ]
         excess = []
         for g in range(GROUP):
-            ratio = held[places[g]].astype(F32) / products[g]
+            ratio = held[start + g].astype(F32) / products[g]
             one = (1.0 - ratio).astype(BF16)
             if g:
                 one = jnp.where(start + g < last, one, jnp.zeros_like(one))
@@ -88,16 +87,12 @@
         ]
         for g in range(GROUP):
             grad[sums[g], :] += terms[g]
-
-        @pl.loop(start, jnp.minimum(start + GROUP, last))
-        def _(place):
-            keep(place, half + place - start).start()
-
-    steps = (last - first + GROUP - 1) // GROUP
-
-    @pl.loop(first + GROUP * jnp.maximum(steps - 2, 0), last)
+        for g in range(GROUP):
+            keep(start + g, half + g).start()
+
+    @pl.loop(GROUP * jnp.maximum(steps - 2, 0), GROUP * steps)
     def _(place):
-        keep(place, (place - first) & (RING - 1)).wait()
+        keep(first + place, place & (RING - 1)).wait()
 
 
 def word_terms(name, order, bounds, counts, words, docs, marks, part=None, kept=None):
@@ -109,14 +104,14 @@
         functools.partial(word_kernel, spec),
         out_shape=[
             jax.ShapeDtypeStruct(((high - low) * edge, words.shape[1]), F32),
-            jax.ShapeDtypeStruct((slots, edge, edge), BF16),
+            pltpu.HBM((slots + GROUP, edge, edge), BF16),
         ],
         in_specs=[SMEM, SMEM, HBM, VMEM, VMEM] + [HBM] * chained,
         out_specs=[VMEM, HBM],
         scratch_shapes=[
-            pltpu.VMEM((slots, edge, edge), counts.dtype),
+            pltpu.VMEM((slots + GROUP, edge, edge), counts.dtype),
             pltpu.VMEM((RING, edge, edge), BF16),
-            pltpu.SemaphoreType.DMA((slots,)),
+            pltpu.SemaphoreType.DMA((slots + GROUP,)),
             pltpu.SemaphoreType.DMA((RING,)),
         ],
         input_output_aliases={5: 1} if chained else {},
@@ -128,59 +123,75 @@
 
 def doc_kernel(spec, order, bounds, kept, *refs):
     edge, marks = spec
-    sides, grad, held, sems = refs[:-3], refs[-3], refs[-2], refs[-1]
+    sides, (grad, words, held, side_sems, sems) = refs[:-5], refs[-5:]
+    rows = sides[0].shape[0]
+    blocks = rows // edge
     total = bounds[marks[-1]]
+    steps = (total + GROUP - 1) // GROUP
+    empty = kept.shape[0]
+    loads = [
+        pltpu.make_async_copy(side, words.at[pl.ds(i * rows, rows)], side_sems.at[i])
+        for i, side in enumerate(sides)
+    ]
+    for load in loads:
+        load.start()
 
     def fetch(place):
         return pltpu.make_async_copy(kept.at[place], held.at[place], sems.at[place])
 
-    @pl.loop(0, total)
+    @pl.loop(0, steps * GROUP)
     def _(place):
         fetch(place).start()
 
+    held[empty] = jnp.zeros(held.shape[1:], held.dtype)
     grad[...] = jnp.zeros_like(grad)
-    for words, first_mark, last_mark in zip(sides, marks, marks[1:]):
-        first, last = bounds[first_mark], bounds[last_mark]
-
-        @pl.loop(0, (last - first + GROUP - 1) // GROUP)
-        def _(step, words=words, first=first, last=last):
-            start = first + GROUP * step
-
-            @pl.loop(start, jnp.minimum(start + GROUP, last))
-            def _(place):
-                fetch(place).wait()
-
-            places = [jnp.minimum(start + g, last - 1) for g in range(GROUP)]
-            parts = [code_parts(order[place]) for place in places]
-            cols = [block_at(doc, edge) for _, _, doc in parts]
-            terms = []
-            for g in range(GROUP):
-                one = held[places[g]]
-                if g:
-                    one = jnp.where(start + g < last, one, jnp.zeros_like(one))
-                rows = block_at(parts[g][1], edge)
-                terms.append(
-                    lax.dot_general(
-                        words[rows, :], one, (((0,), (0,)), ((), ())), preferred_element_type=F32
-                    )
+    for load in loads:
+        load.wait()
+
+    def side_of(place):
+        return sum((place >= bounds[mark]).astype(jnp.int32) for mark in marks[1:-1])
+
+    @pl.loop(0, steps)
+    def _(step):
+        start = GROUP * step
+        for g in range(GROUP):
+            fetch(start + g).wait()
+        cols, terms = [], []
+        for g in range(GROUP):
+            place = jnp.minimum(start + g, total - 1)
+            _, word, doc = code_parts(order[place])
+            one = held[jnp.where(start + g < total, place, empty)]
+            cols.append(block_at(doc, edge))
+            terms.append(
+                lax.dot_general(
+                    words[block_at(word + side_of(place) * blocks, edge), :],
+                    one,
+                    (((0,), (0,)), ((), ())),
+                    preferred_element_type=F32,
                 )
-            for c, term in zip(cols, terms):
-                grad[:, c] += term
+            )
+        for c, term in zip(cols, terms):
+            grad[:, c] += term
 
 
 def doc_terms(order, bounds, kept, sides, marks, width):
-    slots, edge, _ = kept.shape
-    rank = sides[0].shape[1]
+    spots, edge, _ = kept.shape
+    rows, rank = sides[0].shape
     return pl.pallas_call(
         functools.partial(doc_kernel, (edge, marks)),
         out_shape=jax.ShapeDtypeStruct((rank, width), F32),
-        in_specs=[SMEM, SMEM, HBM] + [VMEM] * len(sides),
+        in_specs=[SMEM, SMEM, HBM] + [pl.BlockSpec(memory_space=pl.ANY)] * len(sides),
         out_specs=VMEM,
-        scratch_shapes=[pltpu.VMEM((slots, edge, edge), BF16), pltpu.SemaphoreType.DMA((slots,))],
-        compiler_params=params(16),
+        scratch_shapes=[
+            pltpu.VMEM((len(sides) * rows, rank), BF16),
+            pltpu.VMEM((spots + 1, edge, edge), BF16),
+            pltpu.SemaphoreType.DMA((len(sides),)),
+            pltpu.SemaphoreType.DMA((spots,)),
+        ],
+        compiler_params=params(20),
         cost_estimate=CHEAP,
         name="docs",
-    )(order, bounds, kept, *sides)
+    )(order, bounds, pltpu.with_memory_space_constraint(kept, pltpu.HBM), *sides)
 
 
 def finish_kernel(start, pieces, chained, *refs):
@@ -198,12 +209,12 @@
         copy.wait()
 
 
-def finish(name, own, near, far, start, result=None):
+def finish(name, own, near, far, start, rows, result=None):
     chained = result is not None
     pieces = 4
     return pl.pallas_call(
         functools.partial(finish_kernel, start, pieces, chained),
-        out_shape=jax.ShapeDtypeStruct(own.shape, F32),
+        out_shape=jax.ShapeDtypeStruct((rows, own.shape[1]), F32),
         in_specs=[VMEM] * 3 + [HBM] * chained,
         out_specs=HBM,
         scratch_shapes=[pltpu.VMEM(far.shape, F32), pltpu.SemaphoreType.DMA((pieces,))],
@@ -274,9 +285,9 @@
         doc_factor.shape[1],
     )
     document_gradient, near = lax.optimization_barrier((document_gradient, near))
-    result = finish("finish_a", own, near, far_a.astype(F32), 0)
+    result = finish("finish_a", own, near, far_a.astype(F32), 0, rows)
     result, far_b = lax.optimization_barrier((result, far_b))
-    result = finish("finish_b", own, near, far_b.astype(F32), half, result)
+    result = finish("finish_b", own, near, far_b.astype(F32), half, rows, result)
     return (result, document_gradient)
 
 

time: 80.1 us -> 79.3 us (0.990)
  starting transfers between devices: 25 us -> 23.5 us
  Pallas kernels: 31.1 us -> 32.4 us
    pallas_call x4, Pallas kernels: 17.5 us -> 19.7 us  [word_terms(): pl.pallas_call(functools.partial(word_kernel, spec), out_shape=[jax.Shape...]
    ppermute x3, starting transfers between devices: 24.8 us -> 23.3 us  [across(): return lax.ppermute(block, 'docs', cross_route)]
    ppermute x3, waiting for transfers between devices: 16.1 us -> 15.2 us  [across(): return lax.ppermute(block, 'docs', cross_route)]
    pallas_call x1, Pallas kernels: 10.7 us -> 9.9 us  [doc_terms(): pl.pallas_call(functools.partial(doc_kernel, (edge, marks)), out_shape=ja...]
    unnamed x4 -> x6, local copies, waits for them, and re-layouts: 3.18 us -> 3.18 us
  transfers between devices with their start and end apart: 5 -> 5, of which waited for: 2 -> 3; matrix products, arithmetic and copies ran while one was open for 3% -> 3% of each run, Pallas kernels for 37% -> 39%
where the time goes in v1:
time: 79.3 us; the launch traced here: 78.6 us
  Pallas kernels  32.4 us (41%)
  starting transfers between devices  23.5 us (30%)
  waiting for transfers between devices  15.3 us (19%)
  local copies, waits for them, and re-layouts  3.18 us (4%)
  other arithmetic  2.81 us (4%)
  between operations  1.41 us (2%)
    ppermute x3, starting transfers between devices, across(): return lax.ppermute(block, 'docs', cross_route)  23.3 us
    pallas_call x4, Pallas kernels, word_terms(): pl.pallas_call(functools.partial(word_kernel, spec), out_shape=[jax.Shape...  19.7 us
    ppermute x3, waiting for transfers between devices, across(): return lax.ppermute(block, 'docs', cross_route)  15.2 us
    pallas_call x1, Pallas kernels, doc_terms(): pl.pallas_call(functools.partial(doc_kernel, (edge, marks)), out_shape=ja...  9.9 us
    unnamed x6, local copies, waits for them, and re-layouts  3.18 us
    pallas_call x2, Pallas kernels, finish(): pl.pallas_call(functools.partial(finish_kernel, start, pieces, chained),...  2.88 us
  transfers between devices with their start and end apart: 5, of which 3 were waited for; matrix products, arithmetic and copies ran while one was open for 3% of the time, Pallas kernels for 39%

profile of v1, /device:TPU:0, one launch (start us, length us, event | category | flops | bytes accessed | tf_op | source)
XLA Modules:
  0.0 78.6 jit_solution(5048483242987965418)
XLA Ops:
  0.7 8.9 %collective-permute-start.1 = (bf16[2048,512]{1,0:T(8,128)(2,1)}, bf16[2048,512]{1,0:T(8,128)(2,1)S(1)}, u32[]{:S(2)}, u32[]{:S(2)}) collective-permute-start(bf16[2048,512]{1,0:T(8,128)(2,1)} %refs_0_.1), channel_id=1, source_target_pairs={{0,127},{1,2},{2,1},{3,4},{4,3},{5,6},{6,5},{7,8},{8,7},{9,10},{10... | collective-permute-start | bytes 6291464 | tf_op jit(solution)/shard_map/ppermute | solution.py:258
  10.2 0.7 iota_add_fusion
  10.9 0.1 convert_reduce_fusion.1.bounds
  11.0 0.2 convert_reduce_fusion
  11.2 0.7 multiply_add_fusion
  11.9 0.1 select_reduce_fusion.order
  12.0 1.6 %copy-done = bf16[512,2048]{1,0:T(8,128)(2,1)S(1)} copy-done((bf16[512,2048]{1,0:T(8,128)(2,1)S(1)}, bf16[512,2048]{1,0:T(8,128)(2,1)}, u32[]{:S(2)}) %copy-start) | copy-done | bytes 2097176
  13.6 1.6 %copy-done.2 = bf16[2048,512]{1,0:T(8,128)(2,1)S(1)} copy-done((bf16[2048,512]{1,0:T(8,128)(2,1)S(1)}, bf16[2048,512]{1,0:T(8,128)(2,1)}, u32[]{:S(2)}) %copy-start.2) | copy-done | bytes 2097176
  15.2 4.5 %own.1 = (f32[2048,512]{1,0:T(8,128)S(1)}, bf16[44,256,256]{2,1,0:T(8,128)(2,1)}) custom-call(s32[40]{0:T(128)S(1)} %select_reduce_fusion.order, s32[25]{0:T(128)S(1)} %convert_reduce_fusion.1.bounds, s32[40,256,256]{2,1,0:T(8,128)} %counts.7, bf16[2048,512]{1,0:T(8,128)(2,1)S(1)} %copy-done.2, bf16[512,2048]{1,0:T(8,128)(2,1)S(1)} %copy-done), custom_call_target="tpu_custom_call" | custom-call | flops 1 | bytes 1 | tf_op jit(solution)/shard_map/own/pallas_call | solution.py:103
  19.7 6.3 %partner.1 = (f32[2048,512]{1,0:T(8,128)S(1)}, bf16[44,256,256]{2,1,0:T(8,128)(2,1)}) custom-call(s32[40]{0:T(128)S(1)} %select_reduce_fusion.order, s32[25]{0:T(128)S(1)} %convert_reduce_fusion.1.bounds, s32[40,256,256]{2,1,0:T(8,128)} %counts.7, bf16[2048,512]{1,0:T(8,128)(2,1)} %collective-permute-done.words.refs_1_, ...), custom_call_target="tpu_custom_call", output_to_operand_aliasing={{1}: (5, {})} | custom-call | flops 1 | bytes 1 | tf_op jit(solution)/shard_map/partner/pallas_call | solution.py:103
  26.1 7.4 %collective-permute-done.1.words.refs_2_ = bf16[2048,512]{1,0:T(8,128)(2,1)S(1)} collective-permute-done((bf16[2048,512]{1,0:T(8,128)(2,1)}, bf16[2048,512]{1,0:T(8,128)(2,1)S(1)}, u32[]{:S(2)}, u32[]{:S(2)}) %collective-permute-start.1) | collective-permute-done | bytes 2097184 | tf_op jit(solution)/shard_map/ppermute | solution.py:258
  33.5 3.6 %cross_a.1 = (f32[1024,512]{1,0:T(8,128)S(1)}, bf16[44,256,256]{2,1,0:T(8,128)(2,1)}) custom-call(s32[40]{0:T(128)S(1)} %select_reduce_fusion.order, s32[25]{0:T(128)S(1)} %convert_reduce_fusion.1.bounds, s32[40,256,256]{2,1,0:T(8,128)} %counts.7, bf16[2048,512]{1,0:T(8,128)(2,1)S(1)} %collective-permute-done.1.words.refs_2_, ...), custom_call_target="tpu_custom_call", output_to_operand_aliasing={{1}: (5, {})} | custom-call | flops 1 | bytes 1 | tf_op jit(solution)/shard_map/cross_a/pallas_call | solution.py:103
  37.2 0.3 convert_element_type.20
  37.4 7.3 %collective-permute-start.2 = (f16[1024,512]{1,0:T(8,128)(2,1)S(1)}, f16[1024,512]{1,0:T(8,128)(2,1)S(1)}, u32[]{:S(2)}, u32[]{:S(2)}) collective-permute-start(f16[1024,512]{1,0:T(8,128)(2,1)S(1)} %convert_element_type.20), channel_id=1, source_target_pairs={{0,127},{1,2},{2,1},{3,4},{4,3},{5,6},{6,5},{7,8},{8,7},{9,10},{10... | collective-permute-start | bytes 3145736 | tf_op jit(solution)/shard_map/ppermute | solution.py:258
  44.7 5.2 %cross_b.1 = (f32[1024,512]{1,0:T(8,128)S(1)}, bf16[44,256,256]{2,1,0:T(8,128)(2,1)}) custom-call(s32[40]{0:T(128)S(1)} %select_reduce_fusion.order, s32[25]{0:T(128)S(1)} %convert_reduce_fusion.1.bounds, s32[40,256,256]{2,1,0:T(8,128)} %counts.7, bf16[2048,512]{1,0:T(8,128)(2,1)S(1)} %collective-permute-done.1.words.refs_2_, ...), custom_call_target="tpu_custom_call", output_to_operand_aliasing={{1}: (5, {})} | custom-call | flops 1 | bytes 1 | tf_op jit(solution)/shard_map/cross_b/pallas_call | solution.py:103
  49.9 0.3 convert_element_type.21
  50.2 7.0 %collective-permute-done.2 = f16[1024,512]{1,0:T(8,128)(2,1)S(1)} collective-permute-done((f16[1024,512]{1,0:T(8,128)(2,1)S(1)}, f16[1024,512]{1,0:T(8,128)(2,1)S(1)}, u32[]{:S(2)}, u32[]{:S(2)}) %collective-permute-start.2) | collective-permute-done | bytes 1048608 | tf_op jit(solution)/shard_map/ppermute | solution.py:258
  57.2 7.2 %collective-permute-start.4 = (f16[1024,512]{1,0:T(8,128)(2,1)S(1)}, f16[1024,512]{1,0:T(8,128)(2,1)S(1)}, u32[]{:S(2)}, u32[]{:S(2)}) collective-permute-start(f16[1024,512]{1,0:T(8,128)(2,1)S(1)} %convert_element_type.21), channel_id=1, source_target_pairs={{0,127},{1,2},{2,1},{3,4},{4,3},{5,6},{6,5},{7,8},{8,7},{9,10},{10... | collective-permute-start | bytes 3145736 | tf_op jit(solution)/shard_map/ppermute | solution.py:258
  64.4 9.9 %docs.9 = f32[512,2048]{1,0:T(8,128)} custom-call(s32[40]{0:T(128)S(1)} %select_reduce_fusion.order, s32[25]{0:T(128)S(1)} %convert_reduce_fusion.1.bounds, bf16[44,256,256]{2,1,0:T(8,128)(2,1)} %get-tuple-element.32.kept, bf16[2048,512]{1,0:T(8,128)(2,1)S(1)} %copy-done.2, bf16[2048,512]{1,0:T(8,128)(2,1)} %collective-permute-done.words.refs_1_, ...), custom_call_target="tpu_custom_call" | custom-call | flops 1 | bytes 1 | tf_op jit(solution)/shard_map/docs/pallas_call | solution.py:180
  74.3 0.3 convert_element_type.22.refs_2_
  74.6 1.4 %finish_a.1.refs_3_ = f32[2048,512]{1,0:T(8,128)} custom-call(f32[2048,512]{1,0:T(8,128)S(1)} %get-tuple-element.21.refs_0_, f32[2048,512]{1,0:T(8,128)S(1)} %collective-permute-done.3.refs_1_, f32[1024,512]{1,0:T(8,128)S(1)} %convert_element_type.22.refs_2_), custom_call_target="tpu_custom_call" | custom-call | flops 1 | bytes 1 | tf_op jit(solution)/shard_map/finish_a/pallas_call | solution.py:215
  76.0 0.8 %collective-permute-done.4 = f16[1024,512]{1,0:T(8,128)(2,1)S(1)} collective-permute-done((f16[1024,512]{1,0:T(8,128)(2,1)S(1)}, f16[1024,512]{1,0:T(8,128)(2,1)S(1)}, u32[]{:S(2)}, u32[]{:S(2)}) %collective-permute-start.4) | collective-permute-done | bytes 1048608 | tf_op jit(solution)/shard_map/ppermute | solution.py:258
  76.9 0.3 convert_element_type.23.refs_2_
  77.1 1.4 %finish_b.1 = f32[2048,512]{1,0:T(8,128)} custom-call(f32[2048,512]{1,0:T(8,128)S(1)} %get-tuple-element.21.refs_0_, f32[2048,512]{1,0:T(8,128)S(1)} %collective-permute-done.3.refs_1_, f32[1024,512]{1,0:T(8,128)S(1)} %convert_element_type.23.refs_2_, f32[2048,512]{1,0:T(8,128)} %finish_a.1.refs_3_), custom_call_target="tpu_custom_call", output_to_operand_aliasing={{}: (3, {})} | custom-call | flops 1 | bytes 1 | tf_op jit(solution)/shard_map/finish_b/pallas_call | solution.py:215
  (8 shorter events, 0.2 us)
Async XLA Ops:
  0.6 19.1 %collective-permute-start = (bf16[2048,512]{1,0:T(8,128)(2,1)}, bf16[2048,512]{1,0:T(8,128)(2,1)}, u32[]{:S(2)}, u32[]{:S(2)}) collective-permute-start(bf16[2048,512]{1,0:T(8,128)(2,1)} %refs_0_.1), channel_id=1, source_target_pairs={{0,1},{1,0},{2,3},{3,2},{4,5},{5,4},{6,7},{7,6},{8,9},{9,8},{10,11... | collective-permute-start | bytes 6291464 | tf_op jit(solution)/shard_map/ppermute | solution.py:261
  0.7 32.8 %collective-permute-start.1 = (bf16[2048,512]{1,0:T(8,128)(2,1)}, bf16[2048,512]{1,0:T(8,128)(2,1)S(1)}, u32[]{:S(2)}, u32[]{:S(2)}) collective-permute-start(bf16[2048,512]{1,0:T(8,128)(2,1)} %refs_0_.1), channel_id=1, source_target_pairs={{0,127},{1,2},{2,1},{3,4},{4,3},{5,6},{6,5},{7,8},{8,7},{9,10},{10... | collective-permute-start | bytes 6291464 | tf_op jit(solution)/shard_map/ppermute | solution.py:258
  12.0 1.6 %copy-start = (bf16[512,2048]{1,0:T(8,128)(2,1)S(1)}, bf16[512,2048]{1,0:T(8,128)(2,1)}, u32[]{:S(2)}) copy-start(bf16[512,2048]{1,0:T(8,128)(2,1)} %docs.8) | copy-start | bytes 6291460
  13.6 1.6 %copy-start.2 = (bf16[2048,512]{1,0:T(8,128)(2,1)S(1)}, bf16[2048,512]{1,0:T(8,128)(2,1)}, u32[]{:S(2)}) copy-start(bf16[2048,512]{1,0:T(8,128)(2,1)} %refs_0_.1) | copy-start | bytes 6291460
  15.2 4.5 %copy-start.1 = (bf16[512,2048]{1,0:T(8,128)(2,1)S(1)}, bf16[512,2048]{1,0:T(8,128)(2,1)}, u32[]{:S(2)}) copy-start(bf16[512,2048]{1,0:T(8,128)(2,1)} %docs.8) | copy-start | bytes 6291460
  26.0 48.6 %collective-permute-start.3 = (f32[2048,512]{1,0:T(8,128)S(1)}, f32[2048,512]{1,0:T(8,128)S(1)}, u32[]{:S(2)}, u32[]{:S(2)}) collective-permute-start(f32[2048,512]{1,0:T(8,128)S(1)} %get-tuple-element.33), channel_id=1, source_target_pairs={{0,1},{1,0},{2,3},{3,2},{4,5},{5,4},{6,7},{7,6},{8,9},{9,8},{10,11... | collective-permute-start | bytes 12582920 | tf_op jit(solution)/shard_map/ppermute | solution.py:270
  37.4 19.8 %collective-permute-start.2 = (f16[1024,512]{1,0:T(8,128)(2,1)S(1)}, f16[1024,512]{1,0:T(8,128)(2,1)S(1)}, u32[]{:S(2)}, u32[]{:S(2)}) collective-permute-start(f16[1024,512]{1,0:T(8,128)(2,1)S(1)} %convert_element_type.20), channel_id=1, source_target_pairs={{0,127},{1,2},{2,1},{3,4},{4,3},{5,6},{6,5},{7,8},{8,7},{9,10},{10... | collective-permute-start | bytes 3145736 | tf_op jit(solution)/shard_map/ppermute | solution.py:258
  57.2 19.7 %collective-permute-start.4 = (f16[1024,512]{1,0:T(8,128)(2,1)S(1)}, f16[1024,512]{1,0:T(8,128)(2,1)S(1)}, u32[]{:S(2)}, u32[]{:S(2)}) collective-permute-start(f16[1024,512]{1,0:T(8,128)(2,1)S(1)} %convert_element_type.21), channel_id=1, source_target_pairs={{0,127},{1,2},{2,1},{3,4},{4,3},{5,6},{6,5},{7,8},{8,7},{9,10},{10... | collective-permute-start | bytes 3145736 | tf_op jit(solution)/shard_map/ppermute | solution.py:258

commit v2 on v1

--- a/solution.py
+++ b/solution.py
@@ -67,8 +67,7 @@
                 keep(start + g - 2 * GROUP, half + g).wait()
 
         parts = [code_parts(order[jnp.minimum(start + g, last - 1)]) for g in range(GROUP)]
-        rows = [block_at(word, edge) for _, word, _ in parts]
-        sums = [block_at(word - base, edge) for _, word, _ in parts]
+        rows = [block_at(word - base, edge) for _, word, _ in parts]
         cols = [block_at(doc, edge) for _, _, doc in parts]
         products = [
             jnp.dot(words[r, :], docs[:, c], preferred_element_type=F32) for r, c in zip(rows, cols)
@@ -86,7 +85,7 @@
             for e, c in zip(excess, cols)
         ]
         for g in range(GROUP):
-            grad[sums[g], :] += terms[g]
+            grad[rows[g], :] += terms[g]
         for g in range(GROUP):
             keep(start + g, half + g).start()
 
@@ -95,15 +94,14 @@
         keep(first + place, place & (RING - 1)).wait()
 
 
-def word_terms(name, order, bounds, counts, words, docs, marks, part=None, kept=None):
+def word_terms(name, order, bounds, counts, words, docs, marks, base=0, kept=None):
     slots, edge, _ = counts.shape
     chained = kept is not None
-    low, high = part or (0, words.shape[0] // edge)
-    spec = (edge, marks[0], marks[1], low, chained)
+    spec = (edge, marks[0], marks[1], base, chained)
     return pl.pallas_call(
         functools.partial(word_kernel, spec),
         out_shape=[
-            jax.ShapeDtypeStruct(((high - low) * edge, words.shape[1]), F32),
+            jax.ShapeDtypeStruct(words.shape, F32),
             pltpu.HBM((slots + GROUP, edge, edge), BF16),
         ],
         in_specs=[SMEM, SMEM, HBM, VMEM, VMEM] + [HBM] * chained,
@@ -124,13 +122,13 @@
 def doc_kernel(spec, order, bounds, kept, *refs):
     edge, marks = spec
     sides, (grad, words, held, side_sems, sems) = refs[:-5], refs[-5:]
-    rows = sides[0].shape[0]
-    blocks = rows // edge
+    starts = [sum(side.shape[0] for side in sides[:i]) for i in range(len(sides))]
+    blocks = sides[0].shape[0] // edge
     total = bounds[marks[-1]]
     steps = (total + GROUP - 1) // GROUP
     empty = kept.shape[0]
     loads = [
-        pltpu.make_async_copy(side, words.at[pl.ds(i * rows, rows)], side_sems.at[i])
+        pltpu.make_async_copy(side, words.at[pl.ds(starts[i], side.shape[0])], side_sems.at[i])
         for i, side in enumerate(sides)
     ]
     for load in loads:
@@ -176,14 +174,14 @@
 
 def doc_terms(order, bounds, kept, sides, marks, width):
     spots, edge, _ = kept.shape
-    rows, rank = sides[0].shape
+    rank = sides[0].shape[1]
     return pl.pallas_call(
         functools.partial(doc_kernel, (edge, marks)),
         out_shape=jax.ShapeDtypeStruct((rank, width), F32),
         in_specs=[SMEM, SMEM, HBM] + [pl.BlockSpec(memory_space=pl.ANY)] * len(sides),
         out_specs=VMEM,
         scratch_shapes=[
-            pltpu.VMEM((len(sides) * rows, rank), BF16),
+            pltpu.VMEM((sum(side.shape[0] for side in sides), rank), BF16),
             pltpu.VMEM((spots + 1, edge, edge), BF16),
             pltpu.SemaphoreType.DMA((len(sides),)),
             pltpu.SemaphoreType.DMA((spots,)),
@@ -257,7 +255,10 @@
     def across(block):
         return lax.ppermute(block, "docs", cross_route)
 
-    there = across(word_factor)
+    half_a, half_b, word_factor = lax.optimization_barrier(
+        (word_factor[:half], word_factor[half:], word_factor)
+    )
+    there_a, there_b = across(half_a), across(half_b)
     partner = lax.ppermute(word_factor, "docs", partner_route)
     order, bounds = slot_order(
         block_word, block_docs, block_count[0], position, own_blocks, devices
@@ -266,25 +267,26 @@
     run = functools.partial(word_terms, bounds=bounds, counts=counts, docs=doc_factor)
     own, kept = run("own", order=order, words=word_factor, marks=marks[0:2])
     near, kept = run("partner", order=order, words=partner, marks=marks[1:3], kept=kept)
-    order, near = lax.optimization_barrier((order, near))
+    order, near = lax.optimization_barrier((order, near.astype(F16)))
     near = lax.ppermute(near, "docs", partner_route)
-    far_a, kept = run("cross_a", order=order, words=there, marks=marks[2:4], kept=kept, part=(0, split))
+    far_a, kept = run("cross_a", order=order, words=there_a, marks=marks[2:4], kept=kept)
     order, far_a = lax.optimization_barrier((order, far_a.astype(F16)))
     far_a = across(far_a)
     far_b, kept = run(
-        "cross_b", order=order, words=there, marks=marks[3:5], kept=kept, part=(split, own_blocks)
-    )
-    order, far_b, far_a = lax.optimization_barrier((order, far_b.astype(F16), far_a))
+        "cross_b", order=order, words=there_b, marks=marks[3:5], kept=kept, base=split
+    )
+    order, far_b = lax.optimization_barrier((order, far_b.astype(F16)))
     far_b = across(far_b)
     document_gradient = doc_terms(
         order,
         bounds,
         kept,
-        (word_factor, partner, there),
+        (word_factor, partner, there_a, there_b),
         (0, own_blocks, 2 * own_blocks, 3 * own_blocks),
         doc_factor.shape[1],
     )
     document_gradient, near = lax.optimization_barrier((document_gradient, near))
+    near = near.astype(F32)
     result = finish("finish_a", own, near, far_a.astype(F32), 0, rows)
     result, far_b = lax.optimization_barrier((result, far_b))
     result = finish("finish_b", own, near, far_b.astype(F32), half, rows, result)

time: 79.3 us -> 66.3 us (0.84)
  waiting for transfers between devices: 15.3 us -> 2.79 us
  starting transfers between devices: 23.5 us -> 20.1 us
  Pallas kernels: 32.4 us -> 35.1 us
    ppermute x3 -> x4, waiting for transfers between devices: 15.2 us -> 2.78 us  [across(): return lax.ppermute(block, 'docs', cross_route)]
    ppermute x3 -> x4, starting transfers between devices: 23.3 us -> 20 us  [across(): return lax.ppermute(block, 'docs', cross_route)]
    unnamed x6, local copies, waits for them, and re-layouts: 3.18 us -> 0.01 us
    slice x0 -> x1, local copies, waits for them, and re-layouts: none -> 3.14 us  [on_device(): word_factor[half:]]
    pallas_call x4, Pallas kernels: 19.7 us -> 22.1 us  [word_terms(): pl.pallas_call(functools.partial(word_kernel, spec), out_shape=[jax.Shape...]
    convert_element_type x1 -> x3, other arithmetic: 0.26 us -> 1.36 us  [the longest x1 0.58 us: on_device(): near = near.astype(F32)]
  transfers between devices with their start and end apart: 5 -> 6, of which waited for: 3 -> 2; matrix products, arithmetic and copies ran while one was open for 3% -> 4% of each run, Pallas kernels for 39% -> 52%
where the time goes in v2:
time: 66.3 us; the launch traced here: 65.3 us
  Pallas kernels  35.1 us (53%)
  starting transfers between devices  20.1 us (30%)
  local copies, waits for them, and re-layouts  3.16 us (5%)
  waiting for transfers between devices  2.79 us (4%)
  other arithmetic  2.59 us (4%)
  between operations  1.46 us (2%)
    pallas_call x4, Pallas kernels, word_terms(): pl.pallas_call(functools.partial(word_kernel, spec), out_shape=[jax.Shape...  22.1 us
    ppermute x4, starting transfers between devices, across(): return lax.ppermute(block, 'docs', cross_route)  20 us
    pallas_call x1, Pallas kernels, doc_terms(): pl.pallas_call(functools.partial(doc_kernel, (edge, marks)), out_shape=ja...  10.1 us
    slice x1, local copies, waits for them, and re-layouts, on_device(): word_factor[half:]  3.14 us
    pallas_call x2, Pallas kernels, finish(): pl.pallas_call(functools.partial(finish_kernel, start, pieces, chained),...  2.88 us
    ppermute x4, waiting for transfers between devices, across(): return lax.ppermute(block, 'docs', cross_route)  2.78 us
  transfers between devices with their start and end apart: 6, of which 2 were waited for; matrix products, arithmetic and copies ran while one was open for 4% of the time, Pallas kernels for 52%

profile of v2, /device:TPU:0, one launch (start us, length us, event | category | flops | bytes accessed | tf_op | source)
XLA Modules:
  0.0 65.3 jit_solution(12924227826577920247)
XLA Ops:
  0.7 3.1 %fusion.1 = (bf16[1024,512]{1,0:T(8,128)(2,1)}, bf16[1024,512]{1,0:T(8,128)(2,1)}) fusion(bf16[2048,512]{1,0:T(8,128)(2,1)} %refs_0_), kind=kLoop, calls=%fused_computation.19 | loop fusion | bytes 4194304 | tf_op jit(solution)/shard_map/slice | solution.py:259
  3.8 8.9 %collective-permute-start.1 = (bf16[1024,512]{1,0:T(8,128)(2,1)}, bf16[1024,512]{1,0:T(8,128)(2,1)S(1)}, u32[]{:S(2)}, u32[]{:S(2)}) collective-permute-start(bf16[1024,512]{1,0:T(8,128)(2,1)} %get-tuple-element.28), channel_id=1, source_target_pairs={{0,127},{1,2},{2,1},{3,4},{4,3},{5,6},{6,5},{7,8},{8,7},{9,10},{10... | collective-permute-start | bytes 3145736 | tf_op jit(solution)/shard_map/ppermute | solution.py:256
  12.7 0.0 collective-permute-start.2
  13.4 0.2 convert_reduce_fusion
  13.6 0.1 select_reduce_fusion.order
  13.7 0.1 convert_reduce_fusion.1.bounds
  13.8 6.2 %own.1 = (f32[2048,512]{1,0:T(8,128)S(1)}, bf16[44,256,256]{2,1,0:T(8,128)(2,1)}) custom-call(s32[40]{0:T(128)S(1)} %select_reduce_fusion.order, s32[25]{0:T(128)S(1)} %convert_reduce_fusion.1.bounds, s32[40,256,256]{2,1,0:T(8,128)} %counts.7, bf16[2048,512]{1,0:T(8,128)(2,1)} %refs_0_, bf16[512,2048]{1,0:T(8,128)(2,1)S(1)} %copy-done), custom_call_target="tpu_custom_call" | custom-call | flops 1 | bytes 1 | tf_op jit(solution)/shard_map/own/pallas_call | solution.py:101
  20.1 7.1 %partner.1 = (f32[2048,512]{1,0:T(8,128)S(1)}, bf16[44,256,256]{2,1,0:T(8,128)(2,1)}) custom-call(s32[40]{0:T(128)S(1)} %select_reduce_fusion.order, s32[25]{0:T(128)S(1)} %convert_reduce_fusion.1.bounds, s32[40,256,256]{2,1,0:T(8,128)} %counts.7, bf16[2048,512]{1,0:T(8,128)(2,1)} %collective-permute-done.words.refs_1_, ...), custom_call_target="tpu_custom_call", output_to_operand_aliasing={{1}: (5, {})} | custom-call | flops 1 | bytes 1 | tf_op jit(solution)/shard_map/partner/pallas_call | solution.py:101
  27.2 0.5 convert_element_type.26
  27.7 0.1 collective-permute-start.3
  27.8 4.5 %cross_a.1 = (f32[1024,512]{1,0:T(8,128)S(1)}, bf16[44,256,256]{2,1,0:T(8,128)(2,1)}) custom-call(s32[40]{0:T(128)S(1)} %select_reduce_fusion.order, s32[25]{0:T(128)S(1)} %convert_reduce_fusion.1.bounds, s32[40,256,256]{2,1,0:T(8,128)} %counts.7, bf16[1024,512]{1,0:T(8,128)(2,1)S(1)} %collective-permute-done.1.words.refs_2_, ...), custom_call_target="tpu_custom_call", output_to_operand_aliasing={{1}: (5, {})} | custom-call | flops 1 | bytes 1 | tf_op jit(solution)/shard_map/cross_a/pallas_call | solution.py:101
  32.3 0.3 convert_element_type.27
  32.6 3.9 %collective-permute-start.4 = (f16[1024,512]{1,0:T(8,128)(2,1)S(1)}, f16[1024,512]{1,0:T(8,128)(2,1)S(1)}, u32[]{:S(2)}, u32[]{:S(2)}) collective-permute-start(f16[1024,512]{1,0:T(8,128)(2,1)S(1)} %convert_element_type.27), channel_id=1, source_target_pairs={{0,127},{1,2},{2,1},{3,4},{4,3},{5,6},{6,5},{7,8},{8,7},{9,10},{10... | collective-permute-start | bytes 3145736 | tf_op jit(solution)/shard_map/ppermute | solution.py:256
  36.5 0.2 collective-permute-done.2.words.refs_3_
  36.7 4.3 %cross_b.1 = (f32[1024,512]{1,0:T(8,128)S(1)}, bf16[44,256,256]{2,1,0:T(8,128)(2,1)}) custom-call(s32[40]{0:T(128)S(1)} %select_reduce_fusion.order, s32[25]{0:T(128)S(1)} %convert_reduce_fusion.1.bounds, s32[40,256,256]{2,1,0:T(8,128)} %counts.7, bf16[1024,512]{1,0:T(8,128)(2,1)} %collective-permute-done.2.words.refs_3_, ...), custom_call_target="tpu_custom_call", output_to_operand_aliasing={{1}: (5, {})} | custom-call | flops 1 | bytes 1 | tf_op jit(solution)/shard_map/cross_b/pallas_call | solution.py:101
  41.0 0.3 convert_element_type.28
  41.3 7.2 %collective-permute-start.5 = (f16[1024,512]{1,0:T(8,128)(2,1)S(1)}, f16[1024,512]{1,0:T(8,128)(2,1)S(1)}, u32[]{:S(2)}, u32[]{:S(2)}) collective-permute-start(f16[1024,512]{1,0:T(8,128)(2,1)S(1)} %convert_element_type.28), channel_id=1, source_target_pairs={{0,127},{1,2},{2,1},{3,4},{4,3},{5,6},{6,5},{7,8},{8,7},{9,10},{10... | collective-permute-start | bytes 3145736 | tf_op jit(solution)/shard_map/ppermute | solution.py:256
  48.5 10.1 %docs.9 = f32[512,2048]{1,0:T(8,128)} custom-call(s32[40]{0:T(128)S(1)} %select_reduce_fusion.order, s32[25]{0:T(128)S(1)} %convert_reduce_fusion.1.bounds, bf16[44,256,256]{2,1,0:T(8,128)(2,1)} %get-tuple-element.36.kept, bf16[2048,512]{1,0:T(8,128)(2,1)} %refs_0_, bf16[2048,512]{1,0:T(8,128)(2,1)} %collective-permute-done.words.refs_1_, ...), custom_call_target="tpu_custom_call" | custom-call | flops 1 | bytes 1 | tf_op jit(solution)/shard_map/docs/pallas_call | solution.py:178
  58.7 0.3 convert_element_type.30.refs_2_
  59.0 0.6 convert_element_type.29.refs_1_
  59.5 1.4 %finish_a.1.refs_3_ = f32[2048,512]{1,0:T(8,128)} custom-call(f32[2048,512]{1,0:T(8,128)S(1)} %get-tuple-element.24.refs_0_, f32[2048,512]{1,0:T(8,128)S(1)} %convert_element_type.29.refs_1_, f32[1024,512]{1,0:T(8,128)S(1)} %convert_element_type.30.refs_2_), custom_call_target="tpu_custom_call" | custom-call | flops 1 | bytes 1 | tf_op jit(solution)/shard_map/finish_a/pallas_call | solution.py:213
  61.0 2.5 %collective-permute-done.5 = f16[1024,512]{1,0:T(8,128)(2,1)S(1)} collective-permute-done((f16[1024,512]{1,0:T(8,128)(2,1)S(1)}, f16[1024,512]{1,0:T(8,128)(2,1)S(1)}, u32[]{:S(2)}, u32[]{:S(2)}) %collective-permute-start.5) | collective-permute-done | bytes 1048608 | tf_op jit(solution)/shard_map/ppermute | solution.py:256
  63.5 0.3 convert_element_type.31.refs_2_
  63.8 1.4 %finish_b.1 = f32[2048,512]{1,0:T(8,128)} custom-call(f32[2048,512]{1,0:T(8,128)S(1)} %get-tuple-element.24.refs_0_, f32[2048,512]{1,0:T(8,128)S(1)} %convert_element_type.29.refs_1_, f32[1024,512]{1,0:T(8,128)S(1)} %convert_element_type.31.refs_2_, f32[2048,512]{1,0:T(8,128)} %finish_a.1.refs_3_), custom_call_target="tpu_custom_call", output_to_operand_aliasing={{}: (3, {})} | custom-call | flops 1 | bytes 1 | tf_op jit(solution)/shard_map/finish_b/pallas_call | solution.py:213
  (13 shorter events, 0.1 us)
Async XLA Ops:
  0.6 12.7 %copy-start.2 = (s32[40]{0:T(128)S(1)}, s32[40]{0:T(128)}, u32[]{:S(2)}) copy-start(s32[40]{0:T(128)} %param.9) | copy-start | bytes 484
  0.6 12.9 %copy-start.1 = (s32[40]{0:T(128)S(1)}, s32[40]{0:T(128)}, u32[]{:S(2)}) copy-start(s32[40]{0:T(128)} %param.10) | copy-start | bytes 484
  0.7 13.2 %copy-start = (bf16[512,2048]{1,0:T(8,128)(2,1)S(1)}, bf16[512,2048]{1,0:T(8,128)(2,1)}, u32[]{:S(2)}) copy-start(bf16[512,2048]{1,0:T(8,128)(2,1)} %docs.8) | copy-start | bytes 6291460
  3.8 16.3 %collective-permute-start = (bf16[2048,512]{1,0:T(8,128)(2,1)}, bf16[2048,512]{1,0:T(8,128)(2,1)}, u32[]{:S(2)}, u32[]{:S(2)}) collective-permute-start(bf16[2048,512]{1,0:T(8,128)(2,1)} %refs_0_), channel_id=1, source_target_pairs={{0,1},{1,0},{2,3},{3,2},{4,5},{5,4},{6,7},{7,6},{8,9},{9,8},{10,11... | collective-permute-start | bytes 6291464 | tf_op jit(solution)/shard_map/ppermute | solution.py:262
  3.8 24.0 %collective-permute-start.1 = (bf16[1024,512]{1,0:T(8,128)(2,1)}, bf16[1024,512]{1,0:T(8,128)(2,1)S(1)}, u32[]{:S(2)}, u32[]{:S(2)}) collective-permute-start(bf16[1024,512]{1,0:T(8,128)(2,1)} %get-tuple-element.28), channel_id=1, source_target_pairs={{0,127},{1,2},{2,1},{3,4},{4,3},{5,6},{6,5},{7,8},{8,7},{9,10},{10... | collective-permute-start | bytes 3145736 | tf_op jit(solution)/shard_map/ppermute | solution.py:256
  12.7 24.0 %collective-permute-start.2 = (bf16[1024,512]{1,0:T(8,128)(2,1)}, bf16[1024,512]{1,0:T(8,128)(2,1)}, u32[]{:S(2)}, u32[]{:S(2)}) collective-permute-start(bf16[1024,512]{1,0:T(8,128)(2,1)} %get-tuple-element.32), channel_id=1, source_target_pairs={{0,127},{1,2},{2,1},{3,4},{4,3},{5,6},{6,5},{7,8},{8,7},{9,10},{10... | collective-permute-start | bytes 3145736 | tf_op jit(solution)/shard_map/ppermute | solution.py:256
  27.7 31.2 %collective-permute-start.3 = (f16[2048,512]{1,0:T(8,128)(2,1)S(1)}, f16[2048,512]{1,0:T(8,128)(2,1)S(1)}, u32[]{:S(2)}, u32[]{:S(2)}) collective-permute-start(f16[2048,512]{1,0:T(8,128)(2,1)S(1)} %convert_element_type.26), channel_id=1, source_target_pairs={{0,1},{1,0},{2,3},{3,2},{4,5},{5,4},{6,7},{7,6},{8,9},{9,8},{10,11... | collective-permute-start | bytes 6291464 | tf_op jit(solution)/shard_map/ppermute | solution.py:271
  32.6 26.1 %collective-permute-start.4 = (f16[1024,512]{1,0:T(8,128)(2,1)S(1)}, f16[1024,512]{1,0:T(8,128)(2,1)S(1)}, u32[]{:S(2)}, u32[]{:S(2)}) collective-permute-start(f16[1024,512]{1,0:T(8,128)(2,1)S(1)} %convert_element_type.27), channel_id=1, source_target_pairs={{0,127},{1,2},{2,1},{3,4},{4,3},{5,6},{6,5},{7,8},{8,7},{9,10},{10... | collective-permute-start | bytes 3145736 | tf_op jit(solution)/shard_map/ppermute | solution.py:256
  41.3 22.2 %collective-permute-start.5 = (f16[1024,512]{1,0:T(8,128)(2,1)S(1)}, f16[1024,512]{1,0:T(8,128)(2,1)S(1)}, u32[]{:S(2)}, u32[]{:S(2)}) collective-permute-start(f16[1024,512]{1,0:T(8,128)(2,1)S(1)} %convert_element_type.28), channel_id=1, source_target_pairs={{0,127},{1,2},{2,1},{3,4},{4,3},{5,6},{6,5},{7,8},{8,7},{9,10},{10... | collective-permute-start | bytes 3145736 | tf_op jit(solution)/shard_map/ppermute | solution.py:256

commit v3 on v2

--- a/solution.py
+++ b/solution.py
@@ -29,6 +29,46 @@
 
 def code_parts(code):
     return code & 63, (code >> 6) & 15, code >> 10
+
+
+def halves_kernel(split, pieces, source, low, high, staged, in_sems, out_sems):
+    rows = source.shape[0] // pieces
+    loads, stores = [], []
+    for piece in range(pieces):
+        here = pl.ds(piece * rows, rows)
+        target = low if piece * rows < split else high
+        there = pl.ds(piece * rows - (0 if piece * rows < split else split), rows)
+        loads.append(pltpu.make_async_copy(source.at[here], staged.at[here], in_sems.at[piece]))
+        stores.append(
+            pltpu.make_async_copy(staged.at[here], target.at[there], out_sems.at[piece])
+        )
+        loads[-1].start()
+    for load, store in zip(loads, stores):
+        load.wait()
+        store.start()
+    for store in stores:
+        store.wait()
+
+
+def halves(block, split, pieces):
+    rows, width = block.shape
+    return pl.pallas_call(
+        functools.partial(halves_kernel, split, pieces),
+        out_shape=[
+            pltpu.HBM((split, width), block.dtype),
+            pltpu.HBM((rows - split, width), block.dtype),
+        ],
+        in_specs=[HBM],
+        out_specs=[HBM, HBM],
+        scratch_shapes=[
+            pltpu.VMEM(block.shape, block.dtype),
+            pltpu.SemaphoreType.DMA((pieces,)),
+            pltpu.SemaphoreType.DMA((pieces,)),
+        ],
+        compiler_params=params(4),
+        cost_estimate=CHEAP,
+        name="halves",
+    )(pltpu.with_memory_space_constraint(block, pltpu.HBM))
 
 
 def word_kernel(spec, order, bounds, counts, words, docs, *refs):
@@ -209,7 +249,7 @@
 
 def finish(name, own, near, far, start, rows, result=None):
     chained = result is not None
-    pieces = 4
+    pieces = max(far.shape[0] // 256, 1)
     return pl.pallas_call(
         functools.partial(finish_kernel, start, pieces, chained),
         out_shape=jax.ShapeDtypeStruct((rows, own.shape[1]), F32),
@@ -255,9 +295,8 @@
     def across(block):
         return lax.ppermute(block, "docs", cross_route)
 
-    half_a, half_b, word_factor = lax.optimization_barrier(
-        (word_factor[:half], word_factor[half:], word_factor)
-    )
+    half_a, half_b = halves(word_factor, half, own_blocks)
+    half_a, half_b, word_factor = lax.optimization_barrier((half_a, half_b, word_factor))
     there_a, there_b = across(half_a), across(half_b)
     partner = lax.ppermute(word_factor, "docs", partner_route)
     order, bounds = slot_order(

time: 66.3 us -> 65.4 us (0.986); the launches traced: 65.3 us -> 65.6 us
  Pallas kernels: 35.1 us -> 32.5 us
  waiting for transfers between devices: 2.79 us -> 4.95 us
  other arithmetic: 2.59 us -> 3.94 us
    pallas_call x4, Pallas kernels: 22.1 us -> 18.6 us  [word_terms(): pl.pallas_call(functools.partial(word_kernel, spec), out_shape=[jax.Shape...]
    unnamed x6 -> x8, local copies, waits for them, and re-layouts: 0.01 us -> 3.19 us
    slice x1 -> x0, local copies, waits for them, and re-layouts: 3.14 us -> none  [on_device(): word_factor[half:]]
    pallas_call x0 -> x1, Pallas kernels: none -> 2.4 us  [halves(): pl.pallas_call(functools.partial(halves_kernel, split, pieces), out_shape...]
    ppermute x4, waiting for transfers between devices: 2.78 us -> 4.94 us  [across(): return lax.ppermute(block, 'docs', cross_route)]
    pallas_call x1, Pallas kernels: 10.1 us -> 8.63 us  [doc_terms(): pl.pallas_call(functools.partial(doc_kernel, (edge, marks)), out_shape=ja...]
    ppermute x4, starting transfers between devices: 20 us -> 19.3 us  [across(): return lax.ppermute(block, 'docs', cross_route)]
  transfers between devices with their start and end apart: 6 -> 6, of which waited for: 2 -> 1; matrix products, arithmetic and copies ran while one was open for 4% -> 6% of each run, Pallas kernels for 52% -> 44%
where the time goes in v3:
time: 65.4 us; the launch traced here: 65.6 us
  Pallas kernels  32.5 us (50%)
  starting transfers between devices  19.5 us (30%)
  waiting for transfers between devices  4.95 us (8%)
  other arithmetic  3.94 us (6%)
  local copies, waits for them, and re-layouts  3.19 us (5%)
  between operations  1.45 us (2%)
    ppermute x4, starting transfers between devices, across(): return lax.ppermute(block, 'docs', cross_route)  19.3 us
    pallas_call x4, Pallas kernels, word_terms(): pl.pallas_call(functools.partial(word_kernel, spec), out_shape=[jax.Shape...  18.6 us
    pallas_call x1, Pallas kernels, doc_terms(): pl.pallas_call(functools.partial(doc_kernel, (edge, marks)), out_shape=ja...  8.63 us
    ppermute x4, waiting for transfers between devices, across(): return lax.ppermute(block, 'docs', cross_route)  4.94 us
    unnamed x8, local copies, waits for them, and re-layouts  3.19 us
    pallas_call x2, Pallas kernels, finish(): pl.pallas_call(functools.partial(finish_kernel, start, pieces, chained),...  2.9 us
    pallas_call x1, Pallas kernels, halves(): pl.pallas_call(functools.partial(halves_kernel, split, pieces), out_shape...  2.4 us
  transfers between devices with their start and end apart: 6, of which 1 were waited for; matrix products, arithmetic and copies ran while one was open for 6% of the time, Pallas kernels for 44%

profile of v3, /device:TPU:0, one launch (start us, length us, event | category | flops | bytes accessed | tf_op | source)
XLA Modules:
  0.0 65.6 jit_solution(14992040961421435837)
XLA Ops:
  0.6 2.4 %halves.1 = (bf16[1024,512]{1,0:T(8,128)(2,1)}, bf16[1024,512]{1,0:T(8,128)(2,1)}) custom-call(bf16[2048,512]{1,0:T(8,128)(2,1)} %refs_0_), custom_call_target="tpu_custom_call" | custom-call | flops 1 | bytes 1 | tf_op jit(solution)/shard_map/halves/pallas_call | solution.py:55
  3.1 8.9 %collective-permute-start.1 = (bf16[1024,512]{1,0:T(8,128)(2,1)}, bf16[1024,512]{1,0:T(8,128)(2,1)S(1)}, u32[]{:S(2)}, u32[]{:S(2)}) collective-permute-start(bf16[1024,512]{1,0:T(8,128)(2,1)} %get-tuple-element.32), channel_id=1, source_target_pairs={{0,127},{1,2},{2,1},{3,4},{4,3},{5,6},{6,5},{7,8},{8,7},{9,10},{10... | collective-permute-start | bytes 3145736 | tf_op jit(solution)/shard_map/ppermute | solution.py:296
  12.7 0.7 %iota_add_fusion = (s32[40]{0:T(128)S(1)}, s32[40]{0:T(128)S(1)}, s32[40]{0:T(128)S(1)}, s32[40]{0:T(128)S(1)}) fusion(pred[]{:T(512)S(6)} %eq.36, s32[]{:T(128)} %bitcast.1, s32[40]{0:T(128)} %param.9, s32[]{:T(128)S(6)} %mul.19), kind=kLoop, calls=%fused_computation.17 | loop fusion | flops 1600 | bytes 809 | tf_op jit(solution)/shard_map/add | solution.py:274
  13.4 0.2 convert_reduce_fusion
  13.5 0.7 %multiply_add_fusion = s32[40]{0:T(128)S(1)} fusion(s32[40]{0:T(128)} %param.10, s32[40]{0:T(128)S(1)} %get-tuple-element.51, s32[40]{0:T(128)S(1)} %get-tuple-element.50), kind=kLoop, calls=%fused_computation.16 | loop fusion | flops 240 | bytes 640 | tf_op jit(solution)/shard_map/add | solution.py:276
  14.3 0.1 convert_reduce_fusion.1.bounds
  14.4 1.6 %copy-done = bf16[512,2048]{1,0:T(8,128)(2,1)S(1)} copy-done((bf16[512,2048]{1,0:T(8,128)(2,1)S(1)}, bf16[512,2048]{1,0:T(8,128)(2,1)}, u32[]{:S(2)}) %copy-start) | copy-done | bytes 2097176
  16.0 1.6 %copy-done.2 = bf16[2048,512]{1,0:T(8,128)(2,1)S(1)} copy-done((bf16[2048,512]{1,0:T(8,128)(2,1)S(1)}, bf16[2048,512]{1,0:T(8,128)(2,1)}, u32[]{:S(2)}) %copy-start.2) | copy-done | bytes 2097176
  17.6 5.3 %own.1 = (f32[2048,512]{1,0:T(8,128)S(1)}, bf16[44,256,256]{2,1,0:T(8,128)(2,1)}) custom-call(s32[40]{0:T(128)S(1)} %select_reduce_fusion.order, s32[25]{0:T(128)S(1)} %convert_reduce_fusion.1.bounds, s32[40,256,256]{2,1,0:T(8,128)} %counts.7, bf16[2048,512]{1,0:T(8,128)(2,1)S(1)} %copy-done.2, bf16[512,2048]{1,0:T(8,128)(2,1)S(1)} %copy-done), custom_call_target="tpu_custom_call" | custom-call | flops 1 | bytes 1 | tf_op jit(solution)/shard_map/own/pallas_call | solution.py:141
  23.0 5.3 %partner.1 = (f32[2048,512]{1,0:T(8,128)S(1)}, bf16[44,256,256]{2,1,0:T(8,128)(2,1)}) custom-call(s32[40]{0:T(128)S(1)} %select_reduce_fusion.order, s32[25]{0:T(128)S(1)} %convert_reduce_fusion.1.bounds, s32[40,256,256]{2,1,0:T(8,128)} %counts.7, bf16[2048,512]{1,0:T(8,128)(2,1)S(1)} %collective-permute-done.words.refs_1_, ...), custom_call_target="tpu_custom_call", output_to_operand_aliasing={{1}: (5, {})} | custom-call | flops 1 | bytes 1 | tf_op jit(solution)/shard_map/partner/pallas_call | solution.py:141
  28.3 0.6 convert_element_type.26
  29.0 3.6 %cross_a.1 = (f32[1024,512]{1,0:T(8,128)S(1)}, bf16[44,256,256]{2,1,0:T(8,128)(2,1)}) custom-call(s32[40]{0:T(128)S(1)} %select_reduce_fusion.order, s32[25]{0:T(128)S(1)} %convert_reduce_fusion.1.bounds, s32[40,256,256]{2,1,0:T(8,128)} %counts.7, bf16[1024,512]{1,0:T(8,128)(2,1)S(1)} %collective-permute-done.1.words.refs_2_, ...), custom_call_target="tpu_custom_call", output_to_operand_aliasing={{1}: (5, {})} | custom-call | flops 1 | bytes 1 | tf_op jit(solution)/shard_map/cross_a/pallas_call | solution.py:141
  32.6 0.3 convert_element_type.27
  32.9 6.3 %collective-permute-start.4 = (f16[1024,512]{1,0:T(8,128)(2,1)S(1)}, f16[1024,512]{1,0:T(8,128)(2,1)S(1)}, u32[]{:S(2)}, u32[]{:S(2)}) collective-permute-start(f16[1024,512]{1,0:T(8,128)(2,1)S(1)} %convert_element_type.27), channel_id=1, source_target_pairs={{0,127},{1,2},{2,1},{3,4},{4,3},{5,6},{6,5},{7,8},{8,7},{9,10},{10... | collective-permute-start | bytes 3145736 | tf_op jit(solution)/shard_map/ppermute | solution.py:296
  39.2 4.3 %cross_b.1 = (f32[1024,512]{1,0:T(8,128)S(1)}, bf16[44,256,256]{2,1,0:T(8,128)(2,1)}) custom-call(s32[40]{0:T(128)S(1)} %select_reduce_fusion.order, s32[25]{0:T(128)S(1)} %convert_reduce_fusion.1.bounds, s32[40,256,256]{2,1,0:T(8,128)} %counts.7, bf16[1024,512]{1,0:T(8,128)(2,1)} %collective-permute-done.2.words.refs_3_, ...), custom_call_target="tpu_custom_call", output_to_operand_aliasing={{1}: (5, {})} | custom-call | flops 1 | bytes 1 | tf_op jit(solution)/shard_map/cross_b/pallas_call | solution.py:141
  43.5 0.3 convert_element_type.28
  43.8 4.1 %collective-permute-start.5 = (f16[1024,512]{1,0:T(8,128)(2,1)S(1)}, f16[1024,512]{1,0:T(8,128)(2,1)S(1)}, u32[]{:S(2)}, u32[]{:S(2)}) collective-permute-start(f16[1024,512]{1,0:T(8,128)(2,1)S(1)} %convert_element_type.28), channel_id=1, source_target_pairs={{0,127},{1,2},{2,1},{3,4},{4,3},{5,6},{6,5},{7,8},{8,7},{9,10},{10... | collective-permute-start | bytes 3145736 | tf_op jit(solution)/shard_map/ppermute | solution.py:296
  47.9 8.6 %docs.9 = f32[512,2048]{1,0:T(8,128)} custom-call(s32[40]{0:T(128)S(1)} %select_reduce_fusion.order, s32[25]{0:T(128)S(1)} %convert_reduce_fusion.1.bounds, bf16[44,256,256]{2,1,0:T(8,128)(2,1)} %get-tuple-element.40.kept, bf16[2048,512]{1,0:T(8,128)(2,1)S(1)} %copy-done.3, bf16[2048,512]{1,0:T(8,128)(2,1)S(1)} %collective-permute-done.words.refs_1_, ...), custom_call_target="tpu_custom_call" | custom-call | flops 1 | bytes 1 | tf_op jit(solution)/shard_map/docs/pallas_call | solution.py:218
  56.5 0.3 convert_element_type.30.refs_2_
  56.8 0.6 convert_element_type.29.refs_1_
  57.4 1.5 %finish_a.1.refs_3_ = f32[2048,512]{1,0:T(8,128)} custom-call(f32[2048,512]{1,0:T(8,128)S(1)} %get-tuple-element.28.refs_0_, f32[2048,512]{1,0:T(8,128)S(1)} %convert_element_type.29.refs_1_, f32[1024,512]{1,0:T(8,128)S(1)} %convert_element_type.30.refs_2_), custom_call_target="tpu_custom_call" | custom-call | flops 1 | bytes 1 | tf_op jit(solution)/shard_map/finish_a/pallas_call | solution.py:253
  58.9 4.9 %collective-permute-done.5 = f16[1024,512]{1,0:T(8,128)(2,1)S(1)} collective-permute-done((f16[1024,512]{1,0:T(8,128)(2,1)S(1)}, f16[1024,512]{1,0:T(8,128)(2,1)S(1)}, u32[]{:S(2)}, u32[]{:S(2)}) %collective-permute-start.5) | collective-permute-done | bytes 1048608 | tf_op jit(solution)/shard_map/ppermute | solution.py:296
  63.8 0.3 convert_element_type.31.refs_2_
  64.1 1.4 %finish_b.1 = f32[2048,512]{1,0:T(8,128)} custom-call(f32[2048,512]{1,0:T(8,128)S(1)} %get-tuple-element.28.refs_0_, f32[2048,512]{1,0:T(8,128)S(1)} %convert_element_type.29.refs_1_, f32[1024,512]{1,0:T(8,128)S(1)} %convert_element_type.31.refs_2_, f32[2048,512]{1,0:T(8,128)} %finish_a.1.refs_3_), custom_call_target="tpu_custom_call", output_to_operand_aliasing={{}: (3, {})} | custom-call | flops 1 | bytes 1 | tf_op jit(solution)/shard_map/finish_b/pallas_call | solution.py:253
  (15 shorter events, 0.3 us)
Async XLA Ops:
  3.0 19.9 %collective-permute-start = (bf16[2048,512]{1,0:T(8,128)(2,1)}, bf16[2048,512]{1,0:T(8,128)(2,1)S(1)}, u32[]{:S(2)}, u32[]{:S(2)}) collective-permute-start(bf16[2048,512]{1,0:T(8,128)(2,1)} %refs_0_), channel_id=1, source_target_pairs={{0,1},{1,0},{2,3},{3,2},{4,5},{5,4},{6,7},{7,6},{8,9},{9,8},{10,11... | collective-permute-start | bytes 6291464 | tf_op jit(solution)/shard_map/ppermute | solution.py:301
  3.1 25.8 %collective-permute-start.1 = (bf16[1024,512]{1,0:T(8,128)(2,1)}, bf16[1024,512]{1,0:T(8,128)(2,1)S(1)}, u32[]{:S(2)}, u32[]{:S(2)}) collective-permute-start(bf16[1024,512]{1,0:T(8,128)(2,1)} %get-tuple-element.32), channel_id=1, source_target_pairs={{0,127},{1,2},{2,1},{3,4},{4,3},{5,6},{6,5},{7,8},{8,7},{9,10},{10... | collective-permute-start | bytes 3145736 | tf_op jit(solution)/shard_map/ppermute | solution.py:296
  12.0 27.2 %collective-permute-start.2 = (bf16[1024,512]{1,0:T(8,128)(2,1)}, bf16[1024,512]{1,0:T(8,128)(2,1)}, u32[]{:S(2)}, u32[]{:S(2)}) collective-permute-start(bf16[1024,512]{1,0:T(8,128)(2,1)} %get-tuple-element.36), channel_id=1, source_target_pairs={{0,127},{1,2},{2,1},{3,4},{4,3},{5,6},{6,5},{7,8},{8,7},{9,10},{10... | collective-permute-start | bytes 3145736 | tf_op jit(solution)/shard_map/ppermute | solution.py:296
  14.4 1.6 %copy-start = (bf16[512,2048]{1,0:T(8,128)(2,1)S(1)}, bf16[512,2048]{1,0:T(8,128)(2,1)}, u32[]{:S(2)}) copy-start(bf16[512,2048]{1,0:T(8,128)(2,1)} %docs.8) | copy-start | bytes 6291460
  16.0 1.6 %copy-start.2 = (bf16[2048,512]{1,0:T(8,128)(2,1)S(1)}, bf16[2048,512]{1,0:T(8,128)(2,1)}, u32[]{:S(2)}) copy-start(bf16[2048,512]{1,0:T(8,128)(2,1)} %refs_0_) | copy-start | bytes 6291460
  17.6 5.4 %copy-start.1 = (bf16[512,2048]{1,0:T(8,128)(2,1)S(1)}, bf16[512,2048]{1,0:T(8,128)(2,1)}, u32[]{:S(2)}) copy-start(bf16[512,2048]{1,0:T(8,128)(2,1)} %docs.8) | copy-start | bytes 6291460
  28.9 28.0 %collective-permute-start.3 = (f16[2048,512]{1,0:T(8,128)(2,1)S(1)}, f16[2048,512]{1,0:T(8,128)(2,1)S(1)}, u32[]{:S(2)}, u32[]{:S(2)}) collective-permute-start(f16[2048,512]{1,0:T(8,128)(2,1)S(1)} %convert_element_type.26), channel_id=1, source_target_pairs={{0,1},{1,0},{2,3},{3,2},{4,5},{5,4},{6,7},{7,6},{8,9},{9,8},{10,11... | collective-permute-start | bytes 6291464 | tf_op jit(solution)/shard_map/ppermute | solution.py:310
  32.9 23.7 %collective-permute-start.4 = (f16[1024,512]{1,0:T(8,128)(2,1)S(1)}, f16[1024,512]{1,0:T(8,128)(2,1)S(1)}, u32[]{:S(2)}, u32[]{:S(2)}) collective-permute-start(f16[1024,512]{1,0:T(8,128)(2,1)S(1)} %convert_element_type.27), channel_id=1, source_target_pairs={{0,127},{1,2},{2,1},{3,4},{4,3},{5,6},{6,5},{7,8},{8,7},{9,10},{10... | collective-permute-start | bytes 3145736 | tf_op jit(solution)/shard_map/ppermute | solution.py:296
  43.5 4.4 %copy-start.3 = (bf16[2048,512]{1,0:T(8,128)(2,1)S(1)}, bf16[2048,512]{1,0:T(8,128)(2,1)}, u32[]{:S(2)}) copy-start(bf16[2048,512]{1,0:T(8,128)(2,1)} %refs_0_) | copy-start | bytes 6291460
  43.8 20.0 %collective-permute-start.5 = (f16[1024,512]{1,0:T(8,128)(2,1)S(1)}, f16[1024,512]{1,0:T(8,128)(2,1)S(1)}, u32[]{:S(2)}, u32[]{:S(2)}) collective-permute-start(f16[1024,512]{1,0:T(8,128)(2,1)S(1)} %convert_element_type.28), channel_id=1, source_target_pairs={{0,127},{1,2},{2,1},{3,4},{4,3},{5,6},{6,5},{7,8},{8,7},{9,10},{10... | collective-permute-start | bytes 3145736 | tf_op jit(solution)/shard_map/ppermute | solution.py:296

commit v4 on v2

--- a/solution.py
+++ b/solution.py
@@ -31,11 +31,51 @@
     return code & 63, (code >> 6) & 15, code >> 10
 
 
+def halves_kernel(split, source, low, high, sems):
+    copies = [
+        pltpu.make_async_copy(source.at[pl.ds(0, split)], low, sems.at[0]),
+        pltpu.make_async_copy(
+            source.at[pl.ds(split, source.shape[0] - split)], high, sems.at[1]
+        ),
+    ]
+    for copy in copies:
+        copy.start()
+    for copy in copies:
+        copy.wait()
+
+
+def halves(block, split):
+    rows, width = block.shape
+    return pl.pallas_call(
+        functools.partial(halves_kernel, split),
+        out_shape=[
+            pltpu.VMEM((split, width), block.dtype),
+            pltpu.VMEM((rows - split, width), block.dtype),
+        ],
+        in_specs=[HBM],
+        out_specs=[VMEM, VMEM],
+        scratch_shapes=[pltpu.SemaphoreType.DMA((2,))],
+        compiler_params=params(4),
+        cost_estimate=CHEAP,
+        name="halves",
+    )(pltpu.with_memory_space_constraint(block, pltpu.HBM))
+
+
 def word_kernel(spec, order, bounds, counts, words, docs, *refs):
-    edge, first_mark, last_mark, base, chained = spec
+    edge, first_mark, last_mark, base, chained, loading = spec
     if chained:
         refs = refs[1:]
-    grad, kept, held, staged, sems, out_sems = refs
+    grad, kept, held, staged, sems, out_sems = refs[:6]
+    loads = []
+    if loading:
+        words_here, docs_here, load_sems = refs[6:]
+        loads = [
+            pltpu.make_async_copy(words, words_here, load_sems.at[0]),
+            pltpu.make_async_copy(docs, docs_here, load_sems.at[1]),
+        ]
+        words, docs = words_here, docs_here
+    for load in loads:
+        load.start()
     first, last = bounds[first_mark], bounds[last_mark]
 
     top = order.shape[0] - 1
@@ -53,6 +93,8 @@
         fetch(place).start()
 
     grad[...] = jnp.zeros_like(grad)
+    for load in loads:
+        load.wait()
 
     @pl.loop(0, steps)
     def _(step):
@@ -97,23 +139,32 @@
 def word_terms(name, order, bounds, counts, words, docs, marks, base=0, kept=None):
     slots, edge, _ = counts.shape
     chained = kept is not None
-    spec = (edge, marks[0], marks[1], base, chained)
+    loading = not chained
+    spec = (edge, marks[0], marks[1], base, chained, loading)
+    if loading:
+        words, docs = (pltpu.with_memory_space_constraint(x, pltpu.HBM) for x in (words, docs))
     return pl.pallas_call(
         functools.partial(word_kernel, spec),
         out_shape=[
             jax.ShapeDtypeStruct(words.shape, F32),
             pltpu.HBM((slots + GROUP, edge, edge), BF16),
         ],
-        in_specs=[SMEM, SMEM, HBM, VMEM, VMEM] + [HBM] * chained,
+        in_specs=[SMEM, SMEM, HBM] + [HBM if loading else VMEM] * 2 + [HBM] * chained,
         out_specs=[VMEM, HBM],
         scratch_shapes=[
             pltpu.VMEM((slots + GROUP, edge, edge), counts.dtype),
             pltpu.VMEM((RING, edge, edge), BF16),
             pltpu.SemaphoreType.DMA((slots + GROUP,)),
             pltpu.SemaphoreType.DMA((RING,)),
+        ]
+        + loading
+        * [
+            pltpu.VMEM(words.shape, words.dtype),
+            pltpu.VMEM(docs.shape, docs.dtype),
+            pltpu.SemaphoreType.DMA((2,)),
         ],
         input_output_aliases={5: 1} if chained else {},
-        compiler_params=params(20),
+        compiler_params=params(24 if loading else 20),
         cost_estimate=CHEAP,
         name=name,
     )(order, bounds, counts, words, docs, *([kept] if chained else []))
@@ -209,7 +260,7 @@
 
 def finish(name, own, near, far, start, rows, result=None):
     chained = result is not None
-    pieces = 4
+    pieces = max(far.shape[0] // 256, 1)
     return pl.pallas_call(
         functools.partial(finish_kernel, start, pieces, chained),
         out_shape=jax.ShapeDtypeStruct((rows, own.shape[1]), F32),
@@ -255,9 +306,8 @@
     def across(block):
         return lax.ppermute(block, "docs", cross_route)
 
-    half_a, half_b, word_factor = lax.optimization_barrier(
-        (word_factor[:half], word_factor[half:], word_factor)
-    )
+    half_a, half_b = halves(word_factor, half)
+    half_a, half_b, word_factor = lax.optimization_barrier((half_a, half_b, word_factor))
     there_a, there_b = across(half_a), across(half_b)
     partner = lax.ppermute(word_factor, "docs", partner_route)
     order, bounds = slot_order(

time: 66.3 us -> 66.5 us (level)
  Pallas kernels: 35.1 us -> 38.9 us
  local copies, waits for them, and re-layouts: 3.16 us -> 0.01 us
  other arithmetic: 2.59 us -> 3.94 us
  waiting for transfers between devices: 2.79 us -> 1.73 us
  starting transfers between devices: 20.1 us -> 19.4 us
    slice x1 -> x0, local copies, waits for them, and re-layouts: 3.14 us -> none  [on_device(): word_factor[half:]]
    pallas_call x0 -> x1, Pallas kernels: none -> 2.88 us  [halves(): pl.pallas_call(functools.partial(halves_kernel, split), out_shape=[pltpu....]
    ppermute x4, waiting for transfers between devices: 2.78 us -> 1.72 us  [across(): return lax.ppermute(block, 'docs', cross_route)]
    ppermute x4, starting transfers between devices: 20 us -> 19.2 us  [across(): return lax.ppermute(block, 'docs', cross_route)]
  transfers between devices with their start and end apart: 6 -> 6, of which waited for: 2 -> 1; matrix products, arithmetic and copies ran while one was open for 4% -> 6% of each run, Pallas kernels for 52% -> 53%
where the time goes in v4:
time: 66.5 us; the launch traced here: 65.4 us
  Pallas kernels  38.9 us (58%)
  starting transfers between devices  19.4 us (29%)
  other arithmetic  3.94 us (6%)
  waiting for transfers between devices  1.73 us (3%)
  between operations  1.45 us (2%)
    pallas_call x4, Pallas kernels, word_terms(): pl.pallas_call(functools.partial(word_kernel, spec), out_shape=[jax.Shape...  22.7 us
    ppermute x4, starting transfers between devices, across(): return lax.ppermute(block, 'docs', cross_route)  19.2 us
    pallas_call x1, Pallas kernels, doc_terms(): pl.pallas_call(functools.partial(doc_kernel, (edge, marks)), out_shape=ja...  10.3 us
    pallas_call x2, Pallas kernels, finish(): pl.pallas_call(functools.partial(finish_kernel, start, pieces, chained),...  2.9 us
    pallas_call x1, Pallas kernels, halves(): pl.pallas_call(functools.partial(halves_kernel, split), out_shape=[pltpu....  2.88 us
    ppermute x4, waiting for transfers between devices, across(): return lax.ppermute(block, 'docs', cross_route)  1.72 us
  transfers between devices with their start and end apart: 6, of which 1 were waited for; matrix products, arithmetic and copies ran while one was open for 6% of the time, Pallas kernels for 53%

profile of v4, /device:TPU:0, one launch (start us, length us, event | category | flops | bytes accessed | tf_op | source)
XLA Modules:
  0.0 65.4 jit_solution(1172005582093672144)
XLA Ops:
  0.6 2.9 %halves.1 = (bf16[1024,512]{1,0:T(8,128)(2,1)}, bf16[1024,512]{1,0:T(8,128)(2,1)}) custom-call(bf16[2048,512]{1,0:T(8,128)(2,1)} %refs_0_), custom_call_target="tpu_custom_call" | custom-call | flops 1 | bytes 1 | tf_op jit(solution)/shard_map/halves/pallas_call | solution.py:49
  3.5 0.1 collective-permute-start
  3.6 8.9 %collective-permute-start.1 = (bf16[1024,512]{1,0:T(8,128)(2,1)}, bf16[1024,512]{1,0:T(8,128)(2,1)S(1)}, u32[]{:S(2)}, u32[]{:S(2)}) collective-permute-start(bf16[1024,512]{1,0:T(8,128)(2,1)} %get-tuple-element.32), channel_id=1, source_target_pairs={{0,127},{1,2},{2,1},{3,4},{4,3},{5,6},{6,5},{7,8},{8,7},{9,10},{10... | collective-permute-start | bytes 3145736 | tf_op jit(solution)/shard_map/ppermute | solution.py:307
  13.2 0.7 %iota_add_fusion = (s32[40]{0:T(128)S(1)}, s32[40]{0:T(128)S(1)}, s32[40]{0:T(128)S(1)}, s32[40]{0:T(128)S(1)}) fusion(pred[]{:T(512)S(6)} %eq.36, s32[]{:T(128)} %bitcast.1, s32[40]{0:T(128)} %param.9, s32[]{:T(128)S(6)} %mul.19), kind=kLoop, calls=%fused_computation.17 | loop fusion | flops 1600 | bytes 809 | tf_op jit(solution)/shard_map/add | solution.py:285
  13.8 0.2 convert_reduce_fusion
  14.0 0.7 %multiply_add_fusion = s32[40]{0:T(128)S(1)} fusion(s32[40]{0:T(128)} %param.10, s32[40]{0:T(128)S(1)} %get-tuple-element.51, s32[40]{0:T(128)S(1)} %get-tuple-element.50), kind=kLoop, calls=%fused_computation.16 | loop fusion | flops 240 | bytes 640 | tf_op jit(solution)/shard_map/add | solution.py:287
  14.7 0.1 select_reduce_fusion.order
  14.8 0.1 convert_reduce_fusion.1.bounds
  14.9 7.9 %own.1 = (f32[2048,512]{1,0:T(8,128)S(1)}, bf16[44,256,256]{2,1,0:T(8,128)(2,1)}) custom-call(s32[40]{0:T(128)S(1)} %select_reduce_fusion.order, s32[25]{0:T(128)S(1)} %convert_reduce_fusion.1.bounds, s32[40,256,256]{2,1,0:T(8,128)} %counts.7, bf16[2048,512]{1,0:T(8,128)(2,1)} %refs_0_, bf16[512,2048]{1,0:T(8,128)(2,1)} %docs.8), custom_call_target="tpu_custom_call" | custom-call | flops 1 | bytes 1 | tf_op jit(solution)/shard_map/own/pallas_call | solution.py:146
  22.9 5.2 %partner.1 = (f32[2048,512]{1,0:T(8,128)S(1)}, bf16[44,256,256]{2,1,0:T(8,128)(2,1)}) custom-call(s32[40]{0:T(128)S(1)} %select_reduce_fusion.order, s32[25]{0:T(128)S(1)} %convert_reduce_fusion.1.bounds, s32[40,256,256]{2,1,0:T(8,128)} %counts.7, bf16[2048,512]{1,0:T(8,128)(2,1)S(1)} %collective-permute-done.words.refs_1_, ...), custom_call_target="tpu_custom_call", output_to_operand_aliasing={{1}: (5, {})} | custom-call | flops 1 | bytes 1 | tf_op jit(solution)/shard_map/partner/pallas_call | solution.py:146
  28.1 0.6 convert_element_type.26
  28.8 3.6 %cross_a.1 = (f32[1024,512]{1,0:T(8,128)S(1)}, bf16[44,256,256]{2,1,0:T(8,128)(2,1)}) custom-call(s32[40]{0:T(128)S(1)} %select_reduce_fusion.order, s32[25]{0:T(128)S(1)} %convert_reduce_fusion.1.bounds, s32[40,256,256]{2,1,0:T(8,128)} %counts.7, bf16[1024,512]{1,0:T(8,128)(2,1)S(1)} %collective-permute-done.1.words.refs_2_, ...), custom_call_target="tpu_custom_call", output_to_operand_aliasing={{1}: (5, {})} | custom-call | flops 1 | bytes 1 | tf_op jit(solution)/shard_map/cross_a/pallas_call | solution.py:146
  32.4 0.3 convert_element_type.27
  32.7 4.3 %collective-permute-start.4 = (f16[1024,512]{1,0:T(8,128)(2,1)S(1)}, f16[1024,512]{1,0:T(8,128)(2,1)S(1)}, u32[]{:S(2)}, u32[]{:S(2)}) collective-permute-start(f16[1024,512]{1,0:T(8,128)(2,1)S(1)} %convert_element_type.27), channel_id=1, source_target_pairs={{0,127},{1,2},{2,1},{3,4},{4,3},{5,6},{6,5},{7,8},{8,7},{9,10},{10... | collective-permute-start | bytes 3145736 | tf_op jit(solution)/shard_map/ppermute | solution.py:307
  37.0 6.0 %cross_b.1 = (f32[1024,512]{1,0:T(8,128)S(1)}, bf16[44,256,256]{2,1,0:T(8,128)(2,1)}) custom-call(s32[40]{0:T(128)S(1)} %select_reduce_fusion.order, s32[25]{0:T(128)S(1)} %convert_reduce_fusion.1.bounds, s32[40,256,256]{2,1,0:T(8,128)} %counts.7, bf16[1024,512]{1,0:T(8,128)(2,1)} %collective-permute-done.2.words.refs_3_, ...), custom_call_target="tpu_custom_call", output_to_operand_aliasing={{1}: (5, {})} | custom-call | flops 1 | bytes 1 | tf_op jit(solution)/shard_map/cross_b/pallas_call | solution.py:146
  43.0 0.3 convert_element_type.28
  43.2 6.0 %collective-permute-start.5 = (f16[1024,512]{1,0:T(8,128)(2,1)S(1)}, f16[1024,512]{1,0:T(8,128)(2,1)S(1)}, u32[]{:S(2)}, u32[]{:S(2)}) collective-permute-start(f16[1024,512]{1,0:T(8,128)(2,1)S(1)} %convert_element_type.28), channel_id=1, source_target_pairs={{0,127},{1,2},{2,1},{3,4},{4,3},{5,6},{6,5},{7,8},{8,7},{9,10},{10... | collective-permute-start | bytes 3145736 | tf_op jit(solution)/shard_map/ppermute | solution.py:307
  49.2 10.3 %docs.9 = f32[512,2048]{1,0:T(8,128)} custom-call(s32[40]{0:T(128)S(1)} %select_reduce_fusion.order, s32[25]{0:T(128)S(1)} %convert_reduce_fusion.1.bounds, bf16[44,256,256]{2,1,0:T(8,128)(2,1)} %get-tuple-element.40.kept, bf16[2048,512]{1,0:T(8,128)(2,1)S(1)} %copy-done.1, bf16[2048,512]{1,0:T(8,128)(2,1)S(1)} %collective-permute-done.words.refs_1_, ...), custom_call_target="tpu_custom_call" | custom-call | flops 1 | bytes 1 | tf_op jit(solution)/shard_map/docs/pallas_call | solution.py:229
  59.6 0.3 convert_element_type.30.refs_2_
  59.9 0.6 convert_element_type.29.refs_1_
  60.4 1.5 %finish_a.1.refs_3_ = f32[2048,512]{1,0:T(8,128)} custom-call(f32[2048,512]{1,0:T(8,128)S(1)} %get-tuple-element.28.refs_0_, f32[2048,512]{1,0:T(8,128)S(1)} %convert_element_type.29.refs_1_, f32[1024,512]{1,0:T(8,128)S(1)} %convert_element_type.30.refs_2_), custom_call_target="tpu_custom_call" | custom-call | flops 1 | bytes 1 | tf_op jit(solution)/shard_map/finish_a/pallas_call | solution.py:264
  61.9 1.7 %collective-permute-done.5 = f16[1024,512]{1,0:T(8,128)(2,1)S(1)} collective-permute-done((f16[1024,512]{1,0:T(8,128)(2,1)S(1)}, f16[1024,512]{1,0:T(8,128)(2,1)S(1)}, u32[]{:S(2)}, u32[]{:S(2)}) %collective-permute-start.5) | collective-permute-done | bytes 1048608 | tf_op jit(solution)/shard_map/ppermute | solution.py:307
  63.6 0.3 convert_element_type.31.refs_2_
  63.9 1.4 %finish_b.1 = f32[2048,512]{1,0:T(8,128)} custom-call(f32[2048,512]{1,0:T(8,128)S(1)} %get-tuple-element.28.refs_0_, f32[2048,512]{1,0:T(8,128)S(1)} %convert_element_type.29.refs_1_, f32[1024,512]{1,0:T(8,128)S(1)} %convert_element_type.31.refs_2_, f32[2048,512]{1,0:T(8,128)} %finish_a.1.refs_3_), custom_call_target="tpu_custom_call", output_to_operand_aliasing={{}: (3, {})} | custom-call | flops 1 | bytes 1 | tf_op jit(solution)/shard_map/finish_b/pallas_call | solution.py:264
  (11 shorter events, 0.1 us)
Async XLA Ops:
  3.5 19.3 %collective-permute-start = (bf16[2048,512]{1,0:T(8,128)(2,1)}, bf16[2048,512]{1,0:T(8,128)(2,1)S(1)}, u32[]{:S(2)}, u32[]{:S(2)}) collective-permute-start(bf16[2048,512]{1,0:T(8,128)(2,1)} %refs_0_), channel_id=1, source_target_pairs={{0,1},{1,0},{2,3},{3,2},{4,5},{5,4},{6,7},{7,6},{8,9},{9,8},{10,11... | collective-permute-start | bytes 6291464 | tf_op jit(solution)/shard_map/ppermute | solution.py:312
  3.6 25.2 %collective-permute-start.1 = (bf16[1024,512]{1,0:T(8,128)(2,1)}, bf16[1024,512]{1,0:T(8,128)(2,1)S(1)}, u32[]{:S(2)}, u32[]{:S(2)}) collective-permute-start(bf16[1024,512]{1,0:T(8,128)(2,1)} %get-tuple-element.32), channel_id=1, source_target_pairs={{0,127},{1,2},{2,1},{3,4},{4,3},{5,6},{6,5},{7,8},{8,7},{9,10},{10... | collective-permute-start | bytes 3145736 | tf_op jit(solution)/shard_map/ppermute | solution.py:307
  12.5 24.5 %collective-permute-start.2 = (bf16[1024,512]{1,0:T(8,128)(2,1)}, bf16[1024,512]{1,0:T(8,128)(2,1)}, u32[]{:S(2)}, u32[]{:S(2)}) collective-permute-start(bf16[1024,512]{1,0:T(8,128)(2,1)} %get-tuple-element.36), channel_id=1, source_target_pairs={{0,127},{1,2},{2,1},{3,4},{4,3},{5,6},{6,5},{7,8},{8,7},{9,10},{10... | collective-permute-start | bytes 3145736 | tf_op jit(solution)/shard_map/ppermute | solution.py:307
  14.9 8.0 %copy-start = (bf16[512,2048]{1,0:T(8,128)(2,1)S(1)}, bf16[512,2048]{1,0:T(8,128)(2,1)}, u32[]{:S(2)}) copy-start(bf16[512,2048]{1,0:T(8,128)(2,1)} %docs.8) | copy-start | bytes 6291460
  28.7 31.2 %collective-permute-start.3 = (f16[2048,512]{1,0:T(8,128)(2,1)S(1)}, f16[2048,512]{1,0:T(8,128)(2,1)S(1)}, u32[]{:S(2)}, u32[]{:S(2)}) collective-permute-start(f16[2048,512]{1,0:T(8,128)(2,1)S(1)} %convert_element_type.26), channel_id=1, source_target_pairs={{0,1},{1,0},{2,3},{3,2},{4,5},{5,4},{6,7},{7,6},{8,9},{9,8},{10,11... | collective-permute-start | bytes 6291464 | tf_op jit(solution)/shard_map/ppermute | solution.py:321
  32.7 26.9 %collective-permute-start.4 = (f16[1024,512]{1,0:T(8,128)(2,1)S(1)}, f16[1024,512]{1,0:T(8,128)(2,1)S(1)}, u32[]{:S(2)}, u32[]{:S(2)}) collective-permute-start(f16[1024,512]{1,0:T(8,128)(2,1)S(1)} %convert_element_type.27), channel_id=1, source_target_pairs={{0,127},{1,2},{2,1},{3,4},{4,3},{5,6},{6,5},{7,8},{8,7},{9,10},{10... | collective-permute-start | bytes 3145736 | tf_op jit(solution)/shard_map/ppermute | solution.py:307
  43.0 6.2 %copy-start.1 = (bf16[2048,512]{1,0:T(8,128)(2,1)S(1)}, bf16[2048,512]{1,0:T(8,128)(2,1)}, u32[]{:S(2)}) copy-start(bf16[2048,512]{1,0:T(8,128)(2,1)} %refs_0_) | copy-start | bytes 6291460
  43.2 20.4 %collective-permute-start.5 = (f16[1024,512]{1,0:T(8,128)(2,1)S(1)}, f16[1024,512]{1,0:T(8,128)(2,1)S(1)}, u32[]{:S(2)}, u32[]{:S(2)}) collective-permute-start(f16[1024,512]{1,0:T(8,128)(2,1)S(1)} %convert_element_type.28), channel_id=1, source_target_pairs={{0,127},{1,2},{2,1},{3,4},{4,3},{5,6},{6,5},{7,8},{8,7},{9,10},{10... | collective-permute-start | bytes 3145736 | tf_op jit(solution)/shard_map/ppermute | solution.py:307
